TPU v7x, 512 devices: a whole 4x4x16 slice. The times are simulated.
512 devices in a mesh: gx: 8 (over y, core), gy: 16 (over z), gz: 4 (over x).
Axes of the slice: x: 4, y: 4, z: 16, core: 2. Of those that a mesh axis runs over, the one named last changes fastest.
Arguments:
- history: float32 [56, 32, 128, 1024], P(None, 'gz', 'gy', 'gx'), may hold values from -6 to 6
- start: float32 [4, 32, 128, 1024], P(None, 'gz', 'gy', 'gx'), may hold values from -51 to 51
- diagonal: float32 [32, 128, 1024], P('gz', 'gy', 'gx'), may hold values from 0.25 to 2
Outputs:
- new_basis: float32 [20, 32, 128, 1024], P(None, 'gz', 'gy', 'gx')
- r_factor: float32 [20, 20], replicated
All inputs are finite; a program needn't handle non-finite values.
Results may differ from a plain program's by a relative error of at most 0.0003.
Values sent between devices are 32-bit elements; how exact they have to be, the bound alone decides.
A program may use at most 64 MiB of HBM per device.

v0:
```python
import jax
import jax.numpy as jnp
from jax import lax
from jax.sharding import PartitionSpec as P

STEPS = 4
HIST = 56
COLS = 20


def with_halo(block, sides, width):
    for axis, dim in sides:
        count = lax.axis_size(axis)
        forward = [(i, i + 1) for i in range(count - 1)]
        backward = [(target, source) for source, target in forward]
        low = lax.ppermute(
            lax.slice_in_dim(block, block.shape[dim] - width, None, axis=dim), axis, forward
        )
        high = lax.ppermute(lax.slice_in_dim(block, 0, width, axis=dim), axis, backward)
        block = jnp.concatenate([low, block, high], axis=dim)
    return block


def crop_cells(array, margin):
    return array[
        ...,
        margin : array.shape[-3] - margin,
        margin : array.shape[-2] - margin,
        margin : array.shape[-1] - margin,
    ]


def scaled_from_padded(padded, diag_inner, mask_inner):
    center = crop_cells(padded, 1)
    beside = padded[:, 2:, 1:-1, 1:-1] + padded[:, :-2, 1:-1, 1:-1]
    beside = beside + padded[:, 1:-1, 2:, 1:-1] + padded[:, 1:-1, :-2, 1:-1]
    beside = beside + padded[:, 1:-1, 1:-1, 2:] + padded[:, 1:-1, 1:-1, :-2]
    return ((6.0 + diag_inner[None]) * center - beside - 7.0 * center) / 7.0 * mask_inner


def on_device(history, start, diagonal):
    depth_z, depth_y, depth_x = diagonal.shape

    def scaled_step(field):
        padded = with_halo(field, (("gx", 3), ("gy", 2), ("gz", 1)), 1)
        return scaled_from_padded(padded, diagonal, 1.0)

    blocks = [start, scaled_step(start)]
    for level in range(1, STEPS):
        blocks.append(2.0 * scaled_step(blocks[level]) - blocks[level - 1])
    basis = jnp.concatenate(blocks, axis=0)
    cell_total = float(
        depth_z
        * depth_y
        * depth_x
        * lax.axis_size("gx")
        * lax.axis_size("gy")
        * lax.axis_size("gz")
    )
    flat_basis = basis.reshape(COLS, -1)
    flat_hist = history.reshape(HIST, -1)
    highest = lax.Precision.HIGHEST
    local_coef = jnp.dot(
        flat_hist, flat_basis.T, precision=highest, preferred_element_type=jnp.float32
    )
    coef = lax.psum(local_coef, ("gx", "gy", "gz")) / cell_total
    projected = flat_basis - jnp.dot(
        coef.T, flat_hist, precision=highest, preferred_element_type=jnp.float32
    )
    local_gram = jnp.dot(
        projected, projected.T, precision=highest, preferred_element_type=jnp.float32
    )
    gram = lax.psum(local_gram, ("gx", "gy", "gz")) / cell_total
    lower = jnp.linalg.cholesky(gram)
    solved = lax.linalg.triangular_solve(lower, projected, left_side=True, lower=True)
    return (solved.reshape(basis.shape), lower.T)


def solution(mesh):
    return jax.shard_map(
        on_device,
        mesh=mesh,
        in_specs=(P(None, "gz", "gy", "gx"), P(None, "gz", "gy", "gx"), P("gz", "gy", "gx")),
        out_specs=(P(None, "gz", "gy", "gx"), P()),
        check_vma=False,
    )
```

profile of v0, /device:TPU:1, one launch (start us, length us, event | category | flops | bytes accessed | tf_op | source)
XLA Modules:
  0.0 336.8 jit_solution(8611840169034410942)
XLA Ops:
  0.6 1.1 fusion.57
  1.8 8.8 %collective-permute-start.1 = (f32[4,8,8,1]{3,2,1,0:T(8,128)S(1)}, f32[4,8,8,1]{3,2,1,0:T(8,128)S(1)}, u32[]{:S(2)}, u32[]{:S(2)}) collective-permute-start(f32[4,8,8,1]{3,2,1,0:T(8,128)S(1)} %get-tuple-element.32), channel_id=1, source_target_pairs={{64,0},{128,64},{192,128},{256,192},{320,256},{384,320},{448,384},... | collective-permute-start | bytes 3080 | tf_op jit(solution)/shard_map/ppermute | solution.py:19
  10.6 1.9 collective-permute-start
  12.5 1.9 collective-permute-done
  14.4 1.2 pad_maximum_fusion.101
  15.7 1.3 collective-permute-start.3
  17.0 4.0 %collective-permute-start.2 = (f32[4,8,1,130]{3,2,1,0:T(1,128)S(1)}, f32[4,8,1,130]{3,2,1,0:T(1,128)S(1)}, u32[]{:S(2)}, u32[]{:S(2)}) collective-permute-start(f32[4,8,1,130]{3,2,1,0:T(1,128)S(1)} %get-tuple-element.25), channel_id=1, source_target_pairs={{0,4},{4,8},{8,12},{12,16},{16,20},{20,24},{24,28},{28,32},{32,36}... | collective-permute-start | bytes 49928 | tf_op jit(solution)/shard_map/ppermute | solution.py:16
  21.0 1.0 collective-permute-done.2
  22.0 0.9 pad_maximum_fusion.91
  22.8 1.3 collective-permute-start.4
  24.1 4.0 %collective-permute-start.5 = (f32[4,1,10,130]{3,2,1,0:T(8,128)S(1)}, f32[4,1,10,130]{3,2,1,0:T(8,128)S(1)}, u32[]{:S(2)}, u32[]{:S(2)}) collective-permute-start(f32[4,1,10,130]{3,2,1,0:T(8,128)S(1)} %get-tuple-element.17), channel_id=1, source_target_pairs={{0,1},{1,2},{2,3},{4,5},{5,6},{6,7},{8,9},{9,10},{10,11},{12,13},{... | collective-permute-start | bytes 62408 | tf_op jit(solution)/shard_map/ppermute | solution.py:16
  28.1 0.8 broadcast_multiply_fusion.1
  28.9 0.5 collective-permute-done.5
  29.4 2.1 broadcast_multiply_fusion
  31.7 3.7 %collective-permute-start.7 = (f32[4,8,8,1]{3,2,1,0:T(8,128)S(1)}, f32[4,8,8,1]{3,2,1,0:T(8,128)S(1)}, u32[]{:S(2)}, u32[]{:S(2)}) collective-permute-start(f32[4,8,8,1]{3,2,1,0:T(8,128)S(1)} %get-tuple-element.30), channel_id=1, source_target_pairs={{64,0},{128,64},{192,128},{256,192},{320,256},{384,320},{448,384},... | collective-permute-start | bytes 3080 | tf_op jit(solution)/shard_map/ppermute | solution.py:19
  35.4 4.8 %collective-permute-start.6 = (f32[4,8,8,1]{3,2,1,0:T(8,128)S(1)}, f32[4,8,8,1]{3,2,1,0:T(8,128)S(1)}, u32[]{:S(2)}, u32[]{:S(2)}) collective-permute-start(f32[4,8,8,1]{3,2,1,0:T(8,128)S(1)} %get-tuple-element.31), channel_id=1, source_target_pairs={{0,64},{64,128},{128,192},{192,256},{256,320},{320,384},{384,448},... | collective-permute-start | bytes 3080 | tf_op jit(solution)/shard_map/ppermute | solution.py:16
  40.2 0.7 collective-permute-done.7
  40.9 1.2 collective-permute-done.6
  42.1 0.3 pad_maximum_fusion.98
  42.4 1.3 collective-permute-start.9
  43.7 4.6 %collective-permute-start.8 = (f32[4,8,1,130]{3,2,1,0:T(1,128)S(1)}, f32[4,8,1,130]{3,2,1,0:T(1,128)S(1)}, u32[]{:S(2)}, u32[]{:S(2)}) collective-permute-start(f32[4,8,1,130]{3,2,1,0:T(1,128)S(1)} %get-tuple-element.23), channel_id=1, source_target_pairs={{0,4},{4,8},{8,12},{12,16},{16,20},{20,24},{24,28},{28,32},{32,36}... | collective-permute-start | bytes 49928 | tf_op jit(solution)/shard_map/ppermute | solution.py:16
  48.3 1.0 collective-permute-done.8
  49.4 1.3 collective-permute-start.10
  50.7 4.6 %collective-permute-start.11 = (f32[4,1,10,130]{3,2,1,0:T(8,128)S(1)}, f32[4,1,10,130]{3,2,1,0:T(8,128)S(1)}, u32[]{:S(2)}, u32[]{:S(2)}) collective-permute-start(f32[4,1,10,130]{3,2,1,0:T(8,128)S(1)} %get-tuple-element.15), channel_id=1, source_target_pairs={{0,1},{1,2},{2,3},{4,5},{5,6},{6,7},{8,9},{9,10},{10,11},{12,13},{... | collective-permute-start | bytes 62408 | tf_op jit(solution)/shard_map/ppermute | solution.py:16
  55.4 1.3 collective-permute-done.11
  56.7 0.4 constant_dynamic-update-slice_fusion.1
  57.2 1.9 collective-permute-start.13
  59.1 6.1 %collective-permute-start.12 = (f32[4,8,8,1]{3,2,1,0:T(8,128)S(1)}, f32[4,8,8,1]{3,2,1,0:T(8,128)S(1)}, u32[]{:S(2)}, u32[]{:S(2)}) collective-permute-start(f32[4,8,8,1]{3,2,1,0:T(8,128)S(1)} %get-tuple-element.29), channel_id=1, source_target_pairs={{0,64},{64,128},{128,192},{192,256},{256,320},{320,384},{384,448},... | collective-permute-start | bytes 3080 | tf_op jit(solution)/shard_map/ppermute | solution.py:16
  65.2 0.7 collective-permute-done.13
  65.9 1.2 collective-permute-done.12
  67.1 0.3 pad_maximum_fusion.95
  67.4 1.3 collective-permute-start.15
  68.7 4.6 %collective-permute-start.14 = (f32[4,8,1,130]{3,2,1,0:T(1,128)S(1)}, f32[4,8,1,130]{3,2,1,0:T(1,128)S(1)}, u32[]{:S(2)}, u32[]{:S(2)}) collective-permute-start(f32[4,8,1,130]{3,2,1,0:T(1,128)S(1)} %get-tuple-element.21), channel_id=1, source_target_pairs={{0,4},{4,8},{8,12},{12,16},{16,20},{20,24},{24,28},{28,32},{32,36}... | collective-permute-start | bytes 49928 | tf_op jit(solution)/shard_map/ppermute | solution.py:16
  73.3 1.0 collective-permute-done.14
  74.4 1.4 collective-permute-start.16
  75.8 4.6 %collective-permute-start.17 = (f32[4,1,10,130]{3,2,1,0:T(8,128)S(1)}, f32[4,1,10,130]{3,2,1,0:T(8,128)S(1)}, u32[]{:S(2)}, u32[]{:S(2)}) collective-permute-start(f32[4,1,10,130]{3,2,1,0:T(8,128)S(1)} %get-tuple-element.13), channel_id=1, source_target_pairs={{0,1},{1,2},{2,3},{4,5},{5,6},{6,7},{8,9},{9,10},{10,11},{12,13},{... | collective-permute-start | bytes 62408 | tf_op jit(solution)/shard_map/ppermute | solution.py:16
  80.5 1.3 collective-permute-done.17
  81.8 0.4 constant_dynamic-update-slice_fusion
  82.3 1.9 collective-permute-start.19
  84.3 6.1 %collective-permute-start.18 = (f32[4,8,8,1]{3,2,1,0:T(8,128)S(1)}, f32[4,8,8,1]{3,2,1,0:T(8,128)S(1)}, u32[]{:S(2)}, u32[]{:S(2)}) collective-permute-start(f32[4,8,8,1]{3,2,1,0:T(8,128)S(1)} %get-tuple-element.27), channel_id=1, source_target_pairs={{0,64},{64,128},{128,192},{192,256},{256,320},{320,384},{384,448},... | collective-permute-start | bytes 3080 | tf_op jit(solution)/shard_map/ppermute | solution.py:16
  90.3 0.7 collective-permute-done.19
  91.0 1.2 collective-permute-done.18
  92.2 0.3 pad_maximum_fusion.92
  92.5 1.3 collective-permute-start.21
  93.8 4.6 %collective-permute-start.20 = (f32[4,8,1,130]{3,2,1,0:T(1,128)S(1)}, f32[4,8,1,130]{3,2,1,0:T(1,128)S(1)}, u32[]{:S(2)}, u32[]{:S(2)}) collective-permute-start(f32[4,8,1,130]{3,2,1,0:T(1,128)S(1)} %get-tuple-element.19), channel_id=1, source_target_pairs={{0,4},{4,8},{8,12},{12,16},{16,20},{20,24},{24,28},{28,32},{32,36}... | collective-permute-start | bytes 49928 | tf_op jit(solution)/shard_map/ppermute | solution.py:16
  98.4 1.0 collective-permute-done.20
  99.5 1.3 collective-permute-start.22
  100.8 4.6 %collective-permute-start.23 = (f32[4,1,10,130]{3,2,1,0:T(8,128)S(1)}, f32[4,1,10,130]{3,2,1,0:T(8,128)S(1)}, u32[]{:S(2)}, u32[]{:S(2)}) collective-permute-start(f32[4,1,10,130]{3,2,1,0:T(8,128)S(1)} %get-tuple-element.11), channel_id=1, source_target_pairs={{0,1},{1,2},{2,3},{4,5},{5,6},{6,7},{8,9},{9,10},{10,11},{12,13},{... | collective-permute-start | bytes 62408 | tf_op jit(solution)/shard_map/ppermute | solution.py:16
  105.5 1.3 collective-permute-done.23
  106.8 0.4 fusion.15
  107.2 2.7 fusion.4
  109.9 115.6 %psum.14 = f32[56,20]{0,1:T(8,128)S(1)} all-reduce(f32[56,20]{0,1:T(8,128)S(1)} %fusion.4), channel_id=1, replica_groups=mesh['gx'=8,'gy'=16,'gz'=4] {'gx','gy','gz'}, use_global_device_ids=true, to_apply=%region_0.0 | all-reduce | flops 1120 | bytes 8960 | tf_op jit(solution)/shard_map/psum | solution.py:66
  225.7 0.5 copy.17
  226.1 2.0 convolution_subtract_fusion
  228.1 0.9 fusion.58
  229.1 100.0 %psum.15 = f32[20,20]{0,1:T(8,128)S(1)} all-reduce(f32[20,20]{0,1:T(8,128)S(1)} %fusion.58), channel_id=1, replica_groups=mesh['gx'=8,'gy'=16,'gz'=4] {'gx','gy','gz'}, use_global_device_ids=true, to_apply=%region_1.0 | all-reduce | flops 400 | bytes 3200 | tf_op jit(solution)/shard_map/psum | solution.py:73
  329.2 1.8 cholesky.16
  331.0 0.6 compare_reduce_fusion
  331.7 0.7 fusion.48
  332.3 0.7 copy.10
  333.0 1.5 custom-call.6
  334.6 0.2 copy.19
  334.8 1.1 fusion.8
  335.9 1.0 copy.9
  (27 shorter events, 1.0 us)
Async XLA Ops:
  0.6 47.7 %copy-start.1 = (f32[4,8,8,128]{3,2,1,0:T(8,128)S(1)}, f32[4,8,8,128]{3,2,1,0:T(8,128)}, u32[]{:S(2)}) copy-start(f32[4,8,8,128]{3,2,1,0:T(8,128)} %param.4) | copy-start | bytes 393220
  1.8 10.7 %collective-permute-start.1 = (f32[4,8,8,1]{3,2,1,0:T(8,128)S(1)}, f32[4,8,8,1]{3,2,1,0:T(8,128)S(1)}, u32[]{:S(2)}, u32[]{:S(2)}) collective-permute-start(f32[4,8,8,1]{3,2,1,0:T(8,128)S(1)} %get-tuple-element.32), channel_id=1, source_target_pairs={{64,0},{128,64},{192,128},{256,192},{320,256},{384,320},{448,384},... | collective-permute-start | bytes 3080 | tf_op jit(solution)/shard_map/ppermute | solution.py:19
  10.6 3.9 %collective-permute-start = (f32[4,8,8,1]{3,2,1,0:T(8,128)S(1)}, f32[4,8,8,1]{3,2,1,0:T(8,128)S(1)}, u32[]{:S(2)}, u32[]{:S(2)}) collective-permute-start(f32[4,8,8,1]{3,2,1,0:T(8,128)S(1)} %get-tuple-element.33), channel_id=1, source_target_pairs={{0,64},{64,128},{128,192},{192,256},{256,320},{320,384},{384,448},... | collective-permute-start | bytes 3080 | tf_op jit(solution)/shard_map/ppermute | solution.py:16
  15.7 5.3 %collective-permute-start.3 = (f32[4,8,1,130]{3,2,1,0:T(1,128)S(1)}, f32[4,8,1,130]{3,2,1,0:T(1,128)S(1)}, u32[]{:S(2)}, u32[]{:S(2)}) collective-permute-start(f32[4,8,1,130]{3,2,1,0:T(1,128)S(1)} %get-tuple-element.24), channel_id=1, source_target_pairs={{4,0},{8,4},{12,8},{16,12},{20,16},{24,20},{28,24},{32,28},{36,32}... | collective-permute-start | bytes 49928 | tf_op jit(solution)/shard_map/ppermute | solution.py:19
  17.0 5.0 %collective-permute-start.2 = (f32[4,8,1,130]{3,2,1,0:T(1,128)S(1)}, f32[4,8,1,130]{3,2,1,0:T(1,128)S(1)}, u32[]{:S(2)}, u32[]{:S(2)}) collective-permute-start(f32[4,8,1,130]{3,2,1,0:T(1,128)S(1)} %get-tuple-element.25), channel_id=1, source_target_pairs={{0,4},{4,8},{8,12},{12,16},{16,20},{20,24},{24,28},{28,32},{32,36}... | collective-permute-start | bytes 49928 | tf_op jit(solution)/shard_map/ppermute | solution.py:16
  22.8 6.1 %collective-permute-start.4 = (f32[4,1,10,130]{3,2,1,0:T(8,128)S(1)}, f32[4,1,10,130]{3,2,1,0:T(8,128)S(1)}, u32[]{:S(2)}, u32[]{:S(2)}) collective-permute-start(f32[4,1,10,130]{3,2,1,0:T(8,128)S(1)} %get-tuple-element.16), channel_id=1, source_target_pairs={{1,0},{2,1},{3,2},{5,4},{6,5},{7,6},{9,8},{10,9},{11,10},{13,12},{... | collective-permute-start | bytes 62408 | tf_op jit(solution)/shard_map/ppermute | solution.py:19
  24.1 5.3 %collective-permute-start.5 = (f32[4,1,10,130]{3,2,1,0:T(8,128)S(1)}, f32[4,1,10,130]{3,2,1,0:T(8,128)S(1)}, u32[]{:S(2)}, u32[]{:S(2)}) collective-permute-start(f32[4,1,10,130]{3,2,1,0:T(8,128)S(1)} %get-tuple-element.17), channel_id=1, source_target_pairs={{0,1},{1,2},{2,3},{4,5},{5,6},{6,7},{8,9},{9,10},{10,11},{12,13},{... | collective-permute-start | bytes 62408 | tf_op jit(solution)/shard_map/ppermute | solution.py:16
  31.7 9.3 %collective-permute-start.7 = (f32[4,8,8,1]{3,2,1,0:T(8,128)S(1)}, f32[4,8,8,1]{3,2,1,0:T(8,128)S(1)}, u32[]{:S(2)}, u32[]{:S(2)}) collective-permute-start(f32[4,8,8,1]{3,2,1,0:T(8,128)S(1)} %get-tuple-element.30), channel_id=1, source_target_pairs={{64,0},{128,64},{192,128},{256,192},{320,256},{384,320},{448,384},... | collective-permute-start | bytes 3080 | tf_op jit(solution)/shard_map/ppermute | solution.py:19
  35.4 6.8 %collective-permute-start.6 = (f32[4,8,8,1]{3,2,1,0:T(8,128)S(1)}, f32[4,8,8,1]{3,2,1,0:T(8,128)S(1)}, u32[]{:S(2)}, u32[]{:S(2)}) collective-permute-start(f32[4,8,8,1]{3,2,1,0:T(8,128)S(1)} %get-tuple-element.31), channel_id=1, source_target_pairs={{0,64},{64,128},{128,192},{192,256},{256,320},{320,384},{384,448},... | collective-permute-start | bytes 3080 | tf_op jit(solution)/shard_map/ppermute | solution.py:16
  42.4 5.9 %collective-permute-start.9 = (f32[4,8,1,130]{3,2,1,0:T(1,128)S(1)}, f32[4,8,1,130]{3,2,1,0:T(1,128)S(1)}, u32[]{:S(2)}, u32[]{:S(2)}) collective-permute-start(f32[4,8,1,130]{3,2,1,0:T(1,128)S(1)} %get-tuple-element.22), channel_id=1, source_target_pairs={{4,0},{8,4},{12,8},{16,12},{20,16},{24,20},{28,24},{32,28},{36,32}... | collective-permute-start | bytes 49928 | tf_op jit(solution)/shard_map/ppermute | solution.py:19
  43.7 5.6 %collective-permute-start.8 = (f32[4,8,1,130]{3,2,1,0:T(1,128)S(1)}, f32[4,8,1,130]{3,2,1,0:T(1,128)S(1)}, u32[]{:S(2)}, u32[]{:S(2)}) collective-permute-start(f32[4,8,1,130]{3,2,1,0:T(1,128)S(1)} %get-tuple-element.23), channel_id=1, source_target_pairs={{0,4},{4,8},{8,12},{12,16},{16,20},{20,24},{24,28},{28,32},{32,36}... | collective-permute-start | bytes 49928 | tf_op jit(solution)/shard_map/ppermute | solution.py:16
  49.4 5.9 %collective-permute-start.10 = (f32[4,1,10,130]{3,2,1,0:T(8,128)S(1)}, f32[4,1,10,130]{3,2,1,0:T(8,128)S(1)}, u32[]{:S(2)}, u32[]{:S(2)}) collective-permute-start(f32[4,1,10,130]{3,2,1,0:T(8,128)S(1)} %get-tuple-element.14), channel_id=1, source_target_pairs={{1,0},{2,1},{3,2},{5,4},{6,5},{7,6},{9,8},{10,9},{11,10},{13,12},{... | collective-permute-start | bytes 62408 | tf_op jit(solution)/shard_map/ppermute | solution.py:19
  50.7 5.9 %collective-permute-start.11 = (f32[4,1,10,130]{3,2,1,0:T(8,128)S(1)}, f32[4,1,10,130]{3,2,1,0:T(8,128)S(1)}, u32[]{:S(2)}, u32[]{:S(2)}) collective-permute-start(f32[4,1,10,130]{3,2,1,0:T(8,128)S(1)} %get-tuple-element.15), channel_id=1, source_target_pairs={{0,1},{1,2},{2,3},{4,5},{5,6},{6,7},{8,9},{9,10},{10,11},{12,13},{... | collective-permute-start | bytes 62408 | tf_op jit(solution)/shard_map/ppermute | solution.py:16
  57.2 8.7 %collective-permute-start.13 = (f32[4,8,8,1]{3,2,1,0:T(8,128)S(1)}, f32[4,8,8,1]{3,2,1,0:T(8,128)S(1)}, u32[]{:S(2)}, u32[]{:S(2)}) collective-permute-start(f32[4,8,8,1]{3,2,1,0:T(8,128)S(1)} %get-tuple-element.28), channel_id=1, source_target_pairs={{64,0},{128,64},{192,128},{256,192},{320,256},{384,320},{448,384},... | collective-permute-start | bytes 3080 | tf_op jit(solution)/shard_map/ppermute | solution.py:19
  59.1 8.0 %collective-permute-start.12 = (f32[4,8,8,1]{3,2,1,0:T(8,128)S(1)}, f32[4,8,8,1]{3,2,1,0:T(8,128)S(1)}, u32[]{:S(2)}, u32[]{:S(2)}) collective-permute-start(f32[4,8,8,1]{3,2,1,0:T(8,128)S(1)} %get-tuple-element.29), channel_id=1, source_target_pairs={{0,64},{64,128},{128,192},{192,256},{256,320},{320,384},{384,448},... | collective-permute-start | bytes 3080 | tf_op jit(solution)/shard_map/ppermute | solution.py:16
  67.4 5.9 %collective-permute-start.15 = (f32[4,8,1,130]{3,2,1,0:T(1,128)S(1)}, f32[4,8,1,130]{3,2,1,0:T(1,128)S(1)}, u32[]{:S(2)}, u32[]{:S(2)}) collective-permute-start(f32[4,8,1,130]{3,2,1,0:T(1,128)S(1)} %get-tuple-element.20), channel_id=1, source_target_pairs={{4,0},{8,4},{12,8},{16,12},{20,16},{24,20},{28,24},{32,28},{36,32}... | collective-permute-start | bytes 49928 | tf_op jit(solution)/shard_map/ppermute | solution.py:19
  68.7 5.6 %collective-permute-start.14 = (f32[4,8,1,130]{3,2,1,0:T(1,128)S(1)}, f32[4,8,1,130]{3,2,1,0:T(1,128)S(1)}, u32[]{:S(2)}, u32[]{:S(2)}) collective-permute-start(f32[4,8,1,130]{3,2,1,0:T(1,128)S(1)} %get-tuple-element.21), channel_id=1, source_target_pairs={{0,4},{4,8},{8,12},{12,16},{16,20},{20,24},{24,28},{28,32},{32,36}... | collective-permute-start | bytes 49928 | tf_op jit(solution)/shard_map/ppermute | solution.py:16
  74.4 32.8 %copy-start = (f32[56,8,8,128]{3,2,1,0:T(8,128)S(1)}, f32[56,8,8,128]{3,2,1,0:T(8,128)}, u32[]{:S(2)}) copy-start(f32[56,8,8,128]{3,2,1,0:T(8,128)} %param.3) | copy-start | bytes 5505028
  74.4 6.1 %collective-permute-start.16 = (f32[4,1,10,130]{3,2,1,0:T(8,128)S(1)}, f32[4,1,10,130]{3,2,1,0:T(8,128)S(1)}, u32[]{:S(2)}, u32[]{:S(2)}) collective-permute-start(f32[4,1,10,130]{3,2,1,0:T(8,128)S(1)} %get-tuple-element.12), channel_id=1, source_target_pairs={{1,0},{2,1},{3,2},{5,4},{6,5},{7,6},{9,8},{10,9},{11,10},{13,12},{... | collective-permute-start | bytes 62408 | tf_op jit(solution)/shard_map/ppermute | solution.py:19
  75.8 5.9 %collective-permute-start.17 = (f32[4,1,10,130]{3,2,1,0:T(8,128)S(1)}, f32[4,1,10,130]{3,2,1,0:T(8,128)S(1)}, u32[]{:S(2)}, u32[]{:S(2)}) collective-permute-start(f32[4,1,10,130]{3,2,1,0:T(8,128)S(1)} %get-tuple-element.13), channel_id=1, source_target_pairs={{0,1},{1,2},{2,3},{4,5},{5,6},{6,7},{8,9},{9,10},{10,11},{12,13},{... | collective-permute-start | bytes 62408 | tf_op jit(solution)/shard_map/ppermute | solution.py:16
  82.3 8.7 %collective-permute-start.19 = (f32[4,8,8,1]{3,2,1,0:T(8,128)S(1)}, f32[4,8,8,1]{3,2,1,0:T(8,128)S(1)}, u32[]{:S(2)}, u32[]{:S(2)}) collective-permute-start(f32[4,8,8,1]{3,2,1,0:T(8,128)S(1)} %get-tuple-element.26), channel_id=1, source_target_pairs={{64,0},{128,64},{192,128},{256,192},{320,256},{384,320},{448,384},... | collective-permute-start | bytes 3080 | tf_op jit(solution)/shard_map/ppermute | solution.py:19
  84.3 8.0 %collective-permute-start.18 = (f32[4,8,8,1]{3,2,1,0:T(8,128)S(1)}, f32[4,8,8,1]{3,2,1,0:T(8,128)S(1)}, u32[]{:S(2)}, u32[]{:S(2)}) collective-permute-start(f32[4,8,8,1]{3,2,1,0:T(8,128)S(1)} %get-tuple-element.27), channel_id=1, source_target_pairs={{0,64},{64,128},{128,192},{192,256},{256,320},{320,384},{384,448},... | collective-permute-start | bytes 3080 | tf_op jit(solution)/shard_map/ppermute | solution.py:16
  92.5 5.9 %collective-permute-start.21 = (f32[4,8,1,130]{3,2,1,0:T(1,128)S(1)}, f32[4,8,1,130]{3,2,1,0:T(1,128)S(1)}, u32[]{:S(2)}, u32[]{:S(2)}) collective-permute-start(f32[4,8,1,130]{3,2,1,0:T(1,128)S(1)} %get-tuple-element.18), channel_id=1, source_target_pairs={{4,0},{8,4},{12,8},{16,12},{20,16},{24,20},{28,24},{32,28},{36,32}... | collective-permute-start | bytes 49928 | tf_op jit(solution)/shard_map/ppermute | solution.py:19
  93.8 5.6 %collective-permute-start.20 = (f32[4,8,1,130]{3,2,1,0:T(1,128)S(1)}, f32[4,8,1,130]{3,2,1,0:T(1,128)S(1)}, u32[]{:S(2)}, u32[]{:S(2)}) collective-permute-start(f32[4,8,1,130]{3,2,1,0:T(1,128)S(1)} %get-tuple-element.19), channel_id=1, source_target_pairs={{0,4},{4,8},{8,12},{12,16},{16,20},{20,24},{24,28},{28,32},{32,36}... | collective-permute-start | bytes 49928 | tf_op jit(solution)/shard_map/ppermute | solution.py:16
  99.5 5.9 %collective-permute-start.22 = (f32[4,1,10,130]{3,2,1,0:T(8,128)S(1)}, f32[4,1,10,130]{3,2,1,0:T(8,128)S(1)}, u32[]{:S(2)}, u32[]{:S(2)}) collective-permute-start(f32[4,1,10,130]{3,2,1,0:T(8,128)S(1)} %get-tuple-element.10), channel_id=1, source_target_pairs={{1,0},{2,1},{3,2},{5,4},{6,5},{7,6},{9,8},{10,9},{11,10},{13,12},{... | collective-permute-start | bytes 62408 | tf_op jit(solution)/shard_map/ppermute | solution.py:19
  100.8 5.9 %collective-permute-start.23 = (f32[4,1,10,130]{3,2,1,0:T(8,128)S(1)}, f32[4,1,10,130]{3,2,1,0:T(8,128)S(1)}, u32[]{:S(2)}, u32[]{:S(2)}) collective-permute-start(f32[4,1,10,130]{3,2,1,0:T(8,128)S(1)} %get-tuple-element.11), channel_id=1, source_target_pairs={{0,1},{1,2},{2,3},{4,5},{5,6},{6,7},{8,9},{9,10},{10,11},{12,13},{... | collective-permute-start | bytes 62408 | tf_op jit(solution)/shard_map/ppermute | solution.py:16
where the time goes:
time: 338 us; the launch traced here: 337 us
  blocking collectives  216 us (64%)
  starting transfers between devices  81.2 us (24%)
  waiting for transfers between devices  16.1 us (5%)
  other arithmetic  12.1 us (4%)
  matrix products  6.77 us (2%)
  local copies, waits for them, and re-layouts  3.91 us (1%)
    psum x1, blocking collectives, on_device(): coef = lax.psum(local_coef, ('gx', 'gy', 'gz')) / cell_total  116 us
    psum x1, blocking collectives, on_device(): gram = lax.psum(local_gram, ('gx', 'gy', 'gz')) / cell_total  100 us
    ppermute x12, starting transfers between devices, with_halo(): lax.ppermute(lax.slice_in_dim(block, block.shape[dim] - width, None, axis...  54.4 us
    ppermute x12, starting transfers between devices, with_halo(): lax.ppermute(lax.slice_in_dim(block, 0, width, axis=dim), axis, backward)  26.8 us
    ppermute x12, waiting for transfers between devices, with_halo(): lax.ppermute(lax.slice_in_dim(block, block.shape[dim] - width, None, axis...  13.9 us
  transfers between devices with their start and end apart: 24, of which 15 were waited for; matrix products, arithmetic and copies ran while one was open for 0% of the time, Pallas kernels for 0%

commit v1 on v0

v1 whole, which is shorter than its diff:
```python
import functools

import jax
import jax.numpy as jnp
from jax import lax
from jax.experimental import pallas as pl
from jax.experimental.pallas import tpu as pltpu
from jax.sharding import PartitionSpec as P

STEPS = 4
NRHS = 4
HIST = 56
COLS = 20
MESH = pl.DeviceIdType.MESH
F32 = jnp.float32
BF16 = jnp.bfloat16
NT = (((1,), (1,)), ((), ()))
NN = (((1,), (0,)), ((), ()))
HIGH = lax.Precision.HIGHEST


def iota(shape, dim):
    return lax.broadcasted_iota(jnp.int32, shape, dim)


def split(value):
    top = value.astype(BF16)
    return top, (value - top.astype(F32)).astype(BF16)


def bdot(left, right, dims):
    return lax.dot_general(left, right, dims, preferred_element_type=F32)


def fdot(left, right, dims):
    return lax.dot_general(left, right, dims, precision=HIGH, preferred_element_type=F32)


def keep_same_row(value):
    same = (iota(value.shape, 0) % 8) == (iota(value.shape, 1) % 8)
    masked = jnp.where(same, value, 0.0)
    return jnp.sum(masked.reshape(value.shape[0] // 8, 8, value.shape[1]), axis=1)


class Exchange:
    def __init__(self, axis, count, send, recv):
        self.axis, self.count, self.send, self.recv = axis, count, send, recv
        self.me = lax.axis_index(axis)

    def peer(self, step):
        return lax.rem(self.me + step, self.count)

    def copy(self, step, src, dst):
        return pltpu.make_async_remote_copy(
            src_ref=src,
            dst_ref=dst,
            send_sem=self.send.at[step - 1],
            recv_sem=self.recv.at[self.me],
            device_id={self.axis: self.peer(step)},
            device_id_type=MESH,
        )

    def start(self, src_of, dst):
        for step in range(1, self.count):
            self.copy(step, src_of(self.peer(step)), dst).start()

    def wait_recv(self, slot_of):
        for step in range(1, self.count):
            source = self.peer(step)
            slot = slot_of(source)
            pltpu.make_async_remote_copy(
                src_ref=slot,
                dst_ref=slot,
                send_sem=self.send.at[step - 1],
                recv_sem=self.recv.at[source],
                device_id={self.axis: source},
                device_id_type=MESH,
            ).wait_recv()

    def wait_send(self, src_of, dst):
        for step in range(1, self.count):
            self.copy(step, src_of(self.peer(step)), dst).wait_send()


def total_of(ref, count):
    total = ref[0]
    for place in range(1, count):
        total = total + ref[place]
    return total


def power_kernel(
    nx, ny, nz,
    hist_hbm, start_hbm, diag_hbm,
    xcat, cout, gout,
    wbuf, hbuf, ebuf, halo_z, halo_y, halo_x, pack_y, pack_x,
    gloc, g_x, gs_x, g_z, gs_z, g_y, gs_y, ga_z,
    cloc, c_x, c_z, c_y, cs_y,
    load_sem, hs_sem, hr_sem,
    gxs, gxr, gzs, gzr, gys, gyr, gas, gar, gbs, gbr,
    cxs, cxr, czs, czr, cys, cyr, cas, car,
):
    ix, iy, iz = lax.axis_index("gx"), lax.axis_index("gy"), lax.axis_index("gz")
    load_w = pltpu.make_async_copy(start_hbm, wbuf.at[pl.ds(0, NRHS)], load_sem.at[0])
    load_d = pltpu.make_async_copy(diag_hbm, ebuf, load_sem.at[1])
    load_h = pltpu.make_async_copy(hist_hbm, hbuf, load_sem.at[2])
    load_w.start()
    load_d.start()
    load_h.start()

    for which in range(2):
        edge_x = ix == (0 if which == 0 else nx - 1)
        edge_y = iy == (0 if which == 0 else ny - 1)
        edge_z = iz == (0 if which == 0 else nz - 1)

        @pl.when(edge_x)
        def _():
            for level in range(STEPS):
                halo_x[level, which] = jnp.zeros((8, 128), F32)

        @pl.when(edge_y)
        def _():
            for level in range(STEPS):
                halo_y[level, which] = jnp.zeros((32, 128), F32)

        @pl.when(edge_z)
        def _():
            for level in range(STEPS):
                halo_z[level, which] = jnp.zeros((NRHS, 8, 128), F32)

    barrier = pltpu.get_barrier_semaphore()
    for axis, me, count in (("gz", iz, nz), ("gx", ix, nx), ("gy", iy, ny)):
        for step in range(1, count):
            pl.semaphore_signal(
                barrier, inc=1, device_id={axis: lax.rem(me + step, count)}, device_id_type=MESH
            )

    lane = iota((8, 128), 1)
    row = iota((8, 128), 0)

    def faces(level):
        packed = jnp.zeros((8, 128), F32)
        low_rows, high_rows = [], []
        for f in range(NRHS):
            for z in range(8):
                v = wbuf[NRHS * level + f, z]
                n = 2 * (8 * f + z)
                turned = v if n == 0 else pltpu.roll(v, n, 1)
                packed = jnp.where((lane == n) | (lane == (n + 127) % 128), turned, packed)
                low_rows.append(v[0:1])
                high_rows.append(v[7:8])
        pack_x[level] = packed
        pack_y[level, 0] = jnp.concatenate(low_rows, axis=0)
        pack_y[level, 1] = jnp.concatenate(high_rows, axis=0)

    def halo_copies(level):
        block = pl.ds(NRHS * level, NRHS)
        out = []
        for which, step in ((1, -1), (0, 1)):
            has_x = (ix > 0) if step < 0 else (ix < nx - 1)
            has_y = (iy > 0) if step < 0 else (iy < ny - 1)
            has_z = (iz > 0) if step < 0 else (iz < nz - 1)
            for number, has, axis, me, count, src, dst in (
                (0, has_z, "gz", iz, nz, wbuf.at[block, 0 if step < 0 else 7], halo_z),
                (1, has_y, "gy", iy, ny, pack_y.at[level, 1 - which], halo_y),
                (2, has_x, "gx", ix, nx, pack_x.at[level], halo_x),
            ):
                out.append((
                    has,
                    which,
                    number,
                    pltpu.make_async_remote_copy(
                        src_ref=src,
                        dst_ref=dst.at[level, which],
                        send_sem=hs_sem.at[level, which, number],
                        recv_sem=hr_sem.at[level, which, number],
                        device_id={axis: lax.rem(me + step + count, count)},
                        device_id_type=MESH,
                    ),
                ))
        return out

    def send_halos(level):
        for has, _, _, copy in halo_copies(level):
            @pl.when(has)
            def _():
                copy.start()

    def wait_halos(level):
        for _, which, number, copy in halo_copies(level):
            me, count = ((iz, nz), (iy, ny), (ix, nx))[number]
            has = (me > 0) if which == 0 else (me < count - 1)

            @pl.when(has)
            def _():
                copy.wait_recv()

    def finish_halos(level):
        for has, _, _, copy in halo_copies(level):
            @pl.when(has)
            def _():
                copy.wait_send()

    def keep_split(level):
        for z in range(8):
            block = wbuf[NRHS * level:NRHS * (level + 1), z].reshape(8 * NRHS, 128)
            top, low = split(block)
            rows = pl.ds(8 * (HIST + NRHS * level), 8 * NRHS)
            xcat[rows, 128 * z:128 * (z + 1)] = top
            xcat[rows, 1024 + 128 * z:1024 + 128 * (z + 1)] = low

    def advance(level):
        left, right = halo_x[level, 0], halo_x[level, 1]
        both = jnp.where(lane % 2 == 1, left, right)
        for f in range(NRHS):
            for z in range(8):
                n = 2 * (8 * f + z)
                at = NRHS * level + f
                v = wbuf[at, z]
                turned = both if n == 0 else pltpu.roll(both, 128 - n, 1)
                beside = pltpu.roll(jnp.where(lane == 127, turned, v), 1, 1)
                beside = beside + pltpu.roll(jnp.where(lane == 0, turned, v), 127, 1)
                low = halo_y[level, 0, 8 * f + z:8 * f + z + 1]
                high = halo_y[level, 1, 8 * f + z:8 * f + z + 1]
                beside = beside + jnp.where(row == 0, low, pltpu.roll(v, 1, 0))
                beside = beside + jnp.where(row == 7, high, pltpu.roll(v, 7, 0))
                beside = beside + (halo_z[level, 0, f] if z == 0 else wbuf[at, z - 1])
                beside = beside + (halo_z[level, 1, f] if z == 7 else wbuf[at, z + 1])
                scaled = ebuf[z] * v - beside * (1.0 / 7.0)
                if level > 0:
                    scaled = 2.0 * scaled - wbuf[at - NRHS, z]
                wbuf[at + NRHS, z] = scaled

    load_w.wait()
    faces(0)
    load_d.wait()
    ebuf[...] = (ebuf[...] - 1.0) * (1.0 / 7.0)
    load_h.wait()
    for z in range(8):
        top, low = split(hbuf[:, z].reshape(8 * HIST, 128))
        xcat[0:8 * HIST, 128 * z:128 * (z + 1)] = top
        xcat[0:8 * HIST, 1024 + 128 * z:1024 + 128 * (z + 1)] = low
    keep_split(0)

    pl.semaphore_wait(barrier, (nx - 1) + (ny - 1) + (nz - 1))
    send_halos(0)

    top, low = xcat[0:8 * HIST, 0:1024], xcat[0:8 * HIST, 1024:2048]
    pairs = bdot(top, top, NT) + bdot(top, low, NT) + bdot(low, top, NT)
    rows = keep_same_row(pairs)
    pick = (iota((8 * HIST, 128), 0) // 8) == iota((8 * HIST, 128), 1)
    pick2 = (iota((8 * HIST, 128), 0) // 8) == (iota((8 * HIST, 128), 1) - 64)
    folded = fdot(rows[0:32], pick.astype(F32), NN)
    tail = fdot(rows[32:56], pick2.astype(F32), NN)
    folded = folded + jnp.concatenate([tail, jnp.zeros((8, 128), F32)], axis=0)
    for r in range(32):
        gloc[r] = folded[r:r + 1]

    a, b, c = g_x.shape[1], g_z.shape[1], c_x.shape[1]
    e_gx = Exchange("gx", nx, gxs, gxr)
    e_gz = Exchange("gz", nz, gzs, gzr)
    e_gy = Exchange("gy", ny, gys, gyr)
    e_ga = Exchange("gz", nz, gas, gar)
    e_gb = Exchange("gx", nx, gbs, gbr)
    e_cx = Exchange("gx", nx, cxs, cxr)
    e_cz = Exchange("gz", nz, czs, czr)
    e_cy = Exchange("gy", ny, cys, cyr)
    e_ca = Exchange("gx", nx, cas, car)

    gx_src = lambda peer: gloc.at[pl.ds(a * peer, a)]
    gz_src = lambda peer: gs_x.at[pl.ds(b * peer, b)]
    cx_src = lambda peer: cloc.at[pl.ds(c * peer, c)]

    g_x[ix] = gloc[pl.ds(a * ix, a)]
    e_gx.start(gx_src, g_x.at[ix])

    wait_halos(0)
    advance(0)
    faces(1)
    send_halos(1)
    keep_split(1)
    e_gx.wait_recv(lambda s: g_x.at[s])
    gs_x[...] = total_of(g_x, nx)
    g_z[iz] = gs_x[pl.ds(b * iz, b)]
    e_gz.start(gz_src, g_z.at[iz])

    wait_halos(1)
    advance(1)
    faces(2)
    send_halos(2)
    keep_split(2)
    e_gz.wait_recv(lambda s: g_z.at[s])
    gs_z[...] = total_of(g_z, nz)
    g_y[iy] = gs_z[...]
    e_gy.start(lambda peer: gs_z, g_y.at[iy])

    wait_halos(2)
    advance(2)
    faces(3)
    send_halos(3)
    keep_split(3)

    wait_halos(3)
    advance(3)
    keep_split(4)

    wt = xcat[8 * HIST:8 * (HIST + COLS), 0:1024]
    wl = xcat[8 * HIST:8 * (HIST + COLS), 1024:2048]
    xt, xl = xcat[:, 0:1024], xcat[:, 1024:2048]
    pairs = bdot(xt, wt, NT) + bdot(xt, wl, NT) + bdot(xl, wt, NT)
    rows = keep_same_row(pairs)
    rows = jnp.concatenate([rows, jnp.zeros((128 - HIST - COLS, 8 * COLS), F32)], axis=0)
    pick = iota((24, 8 * COLS), 0) == (iota((24, 8 * COLS), 1) // 8)
    products = fdot(pick.astype(F32), rows, NT)
    for r in range(24):
        cloc[r] = products[r:r + 1]
    c_x[ix] = cloc[pl.ds(c * ix, c)]
    e_cx.start(cx_src, c_x.at[ix])

    e_gy.wait_recv(lambda s: g_y.at[s])
    gs_y[...] = total_of(g_y, ny)
    ga_z[pl.ds(b * iz, b)] = gs_y[...]
    e_ga.start(lambda peer: gs_y, ga_z.at[pl.ds(b * iz, b)])

    e_cx.wait_recv(lambda s: c_x.at[s])
    c_z[iz] = total_of(c_x, nx)
    e_cz.start(lambda peer: c_z.at[iz], c_z.at[iz])

    e_ga.wait_recv(lambda s: ga_z.at[pl.ds(b * s, b)])
    gout[pl.ds(a * ix, a)] = ga_z[...]
    e_gb.start(lambda peer: ga_z, gout.at[pl.ds(a * ix, a)])

    e_cz.wait_recv(lambda s: c_z.at[s])
    c_y[iy] = total_of(c_z, nz)
    e_cy.start(lambda peer: c_y.at[iy], c_y.at[iy])

    e_gb.wait_recv(lambda s: gout.at[pl.ds(a * s, a)])
    for level in range(STEPS):
        finish_halos(level)

    e_cy.wait_recv(lambda s: c_y.at[s])
    cs_y[...] = total_of(c_y, ny)
    cout[pl.ds(c * ix, c)] = cs_y[...]
    e_ca.start(lambda peer: cs_y, cout.at[pl.ds(c * ix, c)])

    e_gx.wait_send(gx_src, g_x.at[ix])
    e_gz.wait_send(gz_src, g_z.at[iz])
    e_gy.wait_send(lambda peer: gs_z, g_y.at[iy])
    e_ga.wait_send(lambda peer: gs_y, ga_z.at[pl.ds(b * iz, b)])
    e_gb.wait_send(lambda peer: ga_z, gout.at[pl.ds(a * ix, a)])
    e_cx.wait_send(cx_src, c_x.at[ix])
    e_cz.wait_send(lambda peer: c_z.at[iz], c_z.at[iz])
    e_cy.wait_send(lambda peer: c_y.at[iy], c_y.at[iy])
    e_ca.wait_recv(lambda s: cout.at[pl.ds(c * s, c)])
    e_ca.wait_send(lambda peer: cs_y, cout.at[pl.ds(c * ix, c)])


def finish_kernel(cells, xcat, cout, gout, new_basis, r_factor):
    lane = iota((24, 128), 1)
    row = iota((24, 128), 0)
    scale = 1.0 / cells
    coef = cout[...].reshape(24, 128) * scale
    folded = gout[...].reshape(32, 128) * scale
    turned = pltpu.roll(folded, 64, 1)
    hist_gram = jnp.concatenate([folded, turned[0:24]], axis=0)
    hist_gram = jnp.where(iota((HIST, 128), 1) < HIST, hist_gram, 0.0)
    coef_h = jnp.where(lane < HIST, coef, 0.0)
    work = fdot(coef_h[:, 0:HIST], hist_gram, NN)
    wide = jnp.concatenate([coef_h, jnp.zeros((104, 128), F32)], axis=0)
    gram = fdot(work - 2.0 * coef_h, wide, NT)
    gram = gram + jnp.where(lane < COLS, pltpu.roll(coef, 128 - HIST, 1), 0.0)
    rhs = jnp.where(lane < HIST, -coef, jnp.where(lane - HIST == row, 1.0, 0.0))

    columns = [jnp.broadcast_to(gram[:, k:k + 1], (24, 128)) for k in range(COLS)]
    lower = jnp.zeros((24, 128), F32)
    for j in range(COLS):
        pivot = jnp.broadcast_to(columns[j][j:j + 1], (24, 128))
        inverse = lax.rsqrt(pivot)
        inverse = inverse * (1.5 - 0.5 * pivot * inverse * inverse)
        column = jnp.where(row >= j, columns[j] * inverse, 0.0)
        lower = jnp.where(lane == j, column, lower)
        solved = jnp.broadcast_to(rhs[j:j + 1], (24, 128)) * inverse
        rhs = jnp.where(row == j, solved, rhs - jnp.where(row > j, column * solved, 0.0))
        for k in range(j + 1, COLS):
            columns[k] = columns[k] - column * jnp.broadcast_to(column[k:k + 1], (24, 128))
    square = jnp.concatenate([lower, jnp.zeros((104, 128), F32)], axis=0)
    r_factor[...] = square.T[0:COLS, 0:COLS]

    weights = rhs[0:COLS]
    top, low = split(weights)
    spread = ((iota((128, 8 * (HIST + COLS)), 1) // 8) == iota((128, 8 * (HIST + COLS)), 0)).astype(BF16)
    size = (8 * COLS, 8 * (HIST + COLS))
    same = (iota(size, 0) % 8) == (iota(size, 1) % 8)

    def widen(part):
        wide = bdot(part, spread, NN)
        wide = jnp.broadcast_to(wide[:, None, :], (COLS, 8, size[1])).reshape(size)
        return jnp.where(same, wide, 0.0).astype(BF16)

    top, low = widen(top), widen(low)
    for part in range(4):
        cols = slice(256 * part, 256 * (part + 1))
        lows = slice(1024 + 256 * part, 1024 + 256 * (part + 1))
        out = bdot(top, xcat[:, cols], NN) + bdot(top, xcat[:, lows], NN) + bdot(low, xcat[:, cols], NN)
        for half in range(2):
            new_basis[:, 2 * part + half] = out[:, 128 * half:128 * (half + 1)].reshape(COLS, 8, 128)


def on_device(nx, ny, nz, history, start, diagonal):
    a = 32 // nx
    b = a // nz
    c = 24 // nx
    dma = pltpu.SemaphoreType.DMA
    row = lambda *shape: pltpu.VMEM((*shape, 1, 128), F32)
    any_spec = pl.BlockSpec(memory_space=pl.ANY)
    vmem = pl.BlockSpec(memory_space=pltpu.VMEM)
    xcat, cout, gout = pl.pallas_call(
        functools.partial(power_kernel, nx, ny, nz),
        name="powers",
        out_shape=(
            jax.ShapeDtypeStruct((8 * (HIST + COLS), 2048), BF16),
            jax.ShapeDtypeStruct((24, 1, 128), F32),
            jax.ShapeDtypeStruct((32, 1, 128), F32),
        ),
        in_specs=[any_spec] * 3,
        out_specs=(vmem, vmem, vmem),
        scratch_shapes=[
            pltpu.VMEM((COLS, 8, 8, 128), F32),
            pltpu.VMEM((HIST, 8, 8, 128), F32),
            pltpu.VMEM((8, 8, 128), F32),
            pltpu.VMEM((STEPS, 2, NRHS, 8, 128), F32),
            pltpu.VMEM((STEPS, 2, 32, 128), F32),
            pltpu.VMEM((STEPS, 2, 8, 128), F32),
            pltpu.VMEM((STEPS, 2, 32, 128), F32),
            pltpu.VMEM((STEPS, 8, 128), F32),
            row(32), row(nx, a), row(a), row(nz, b), row(b), row(ny, b), row(b), row(a),
            row(24), row(nx, c), row(nz, c), row(ny, c), row(c),
            dma((3,)), dma((STEPS, 2, 3)), dma((STEPS, 2, 3)),
            dma((nx,)), dma((nx,)), dma((nz,)), dma((nz,)), dma((ny,)), dma((ny,)),
            dma((nz,)), dma((nz,)), dma((nx,)), dma((nx,)),
            dma((nx,)), dma((nx,)), dma((nz,)), dma((nz,)), dma((ny,)), dma((ny,)),
            dma((nx,)), dma((nx,)),
        ],
        compiler_params=pltpu.CompilerParams(
            collective_id=0, has_side_effects=True, vmem_limit_bytes=24 * 1024 * 1024
        ),
    )(history, start, diagonal)
    cells = float(nx * ny * nz * diagonal.size)
    return pl.pallas_call(
        functools.partial(finish_kernel, cells),
        name="finish",
        out_shape=(
            jax.ShapeDtypeStruct((COLS, 8, 8, 128), F32),
            jax.ShapeDtypeStruct((COLS, COLS), F32),
        ),
        in_specs=[vmem] * 3,
        out_specs=(vmem, vmem),
        compiler_params=pltpu.CompilerParams(vmem_limit_bytes=24 * 1024 * 1024),
    )(xcat, cout, gout)


def solution(mesh):
    return jax.shard_map(
        functools.partial(on_device, mesh.shape["gx"], mesh.shape["gy"], mesh.shape["gz"]),
        mesh=mesh,
        in_specs=(P(None, "gz", "gy", "gx"), P(None, "gz", "gy", "gx"), P("gz", "gy", "gx")),
        out_specs=(P(None, "gz", "gy", "gx"), P()),
        check_vma=False,
    )
```

time: 338 us -> 59.3 us (0.18)
  blocking collectives: 216 us -> 0 us
  starting transfers between devices: 81.2 us -> 0 us
  Pallas kernels: 0 us -> 55.2 us
  waiting for transfers between devices: 16.1 us -> 0 us
  other arithmetic: 12.1 us -> 0 us
  matrix products: 6.77 us -> 0 us
    psum x2 -> x0, blocking collectives: 216 us -> none  [the longest x1 116 us: on_device(): coef = lax.psum(local_coef, ('gx', 'gy', 'gz')) / cell_total]
    ppermute x24 -> x0, starting transfers between devices: 81.2 us -> none  [the longest x12 54.4 us: with_halo(): lax.ppermute(lax.slice_in_dim(block, block.shape[dim] - width, None, axis...]
    pallas_call x0 -> x2, Pallas kernels: none -> 55.2 us  [the longest x1 52.5 us: on_device(): pl.pallas_call(functools.partial(power_kernel, nx, ny, nz), name='powers'...]
    ppermute x24 -> x0, waiting for transfers between devices: 16.1 us -> none  [the longest x12 13.9 us: with_halo(): lax.ppermute(lax.slice_in_dim(block, block.shape[dim] - width, None, axis...]
    dot_general x3 -> x0, matrix products: 5.67 us -> none  [the longest x1 2.73 us: on_device(): jnp.dot(flat_hist, flat_basis.T, precision=highest, preferred_element_typ...]
    another operation x4 -> x0, other arithmetic: 4.02 us -> none  [the longest x3 2.49 us: on_device(): lower = jnp.linalg.cholesky(gram)]
  transfers between devices with their start and end apart: 24 -> 0, of which waited for: 15 -> 0; matrix products, arithmetic and copies ran while one was open for 0% -> 0% of each run, Pallas kernels for 0% -> 0%
where the time goes in v1:
time: 59.3 us; the launch traced here: 59.1 us
  Pallas kernels  55.2 us (93%)
  local copies, waits for them, and re-layouts  3.15 us (5%)
  between operations  0.65 us (1%)
    pallas_call x1, Pallas kernels, on_device(): pl.pallas_call(functools.partial(power_kernel, nx, ny, nz), name='powers'...  52.5 us
    unnamed x6, local copies, waits for them, and re-layouts  3.15 us
    pallas_call x1, Pallas kernels, on_device(): pl.pallas_call(functools.partial(finish_kernel, cells), name='finish', ou...  2.74 us

profile of v1, /device:TPU:1, one launch (start us, length us, event | category | flops | bytes accessed | tf_op | source)
XLA Modules:
  0.0 59.1 jit_solution(18318709966337768250)
XLA Ops:
  0.6 0.0 copy-start
  0.6 1.5 %copy-done = f32[56,8,8,128]{3,2,1,0:T(8,128)S(1)} copy-done((f32[56,8,8,128]{3,2,1,0:T(8,128)S(1)}, f32[56,8,8,128]{3,2,1,0:T(8,128)}, u32[]{:S(2)}) %copy-start) | copy-done | bytes 1835032
  2.1 0.0 copy-start.1
  2.1 0.9 %copy-done.1 = f32[4,8,8,128]{3,2,1,0:T(8,128)S(1)} copy-done((f32[4,8,8,128]{3,2,1,0:T(8,128)S(1)}, f32[4,8,8,128]{3,2,1,0:T(8,128)}, u32[]{:S(2)}) %copy-start.1) | copy-done | bytes 131096
  3.0 0.0 copy-start.2
  3.0 0.8 %copy-done.2 = f32[8,8,128]{2,1,0:T(8,128)S(1)} copy-done((f32[8,8,128]{2,1,0:T(8,128)S(1)}, f32[8,8,128]{2,1,0:T(8,128)}, u32[]{:S(2)}) %copy-start.2) | copy-done | bytes 32792
  3.8 52.5 %powers.1 = (bf16[608,2048]{1,0:T(8,128)(2,1)S(1)}, f32[24,1,128]{2,1,0:T(1,128)S(1)}, f32[32,1,128]{2,1,0:T(1,128)S(1)}) custom-call(f32[56,8,8,128]{3,2,1,0:T(8,128)S(1)} %copy-done, f32[4,8,8,128]{3,2,1,0:T(8,128)S(1)} %copy-done.1, f32[8,8,128]{2,1,0:T(8,128)S(1)} %copy-done.2), custom_call_target="tpu_custom_call" | custom-call | tf_op jit(solution)/shard_map/powers/pallas_call | solution.py:417
  56.3 2.7 %finish.1 = (f32[20,8,8,128]{3,2,1,0:T(8,128)}, f32[20,20]{1,0:T(8,128)}) custom-call(bf16[608,2048]{1,0:T(8,128)(2,1)S(1)} %get-tuple-element.5.xcat, f32[24,1,128]{2,1,0:T(1,128)S(1)} %get-tuple-element.6.cout, f32[32,1,128]{2,1,0:T(1,128)S(1)} %get-tuple-element.7.gout), custom_call_target="tpu_custom_call" | custom-call | tf_op jit(solution)/shard_map/finish/pallas_call | solution.py:449
Async XLA Ops:
  0.6 1.5 %copy-start = (f32[56,8,8,128]{3,2,1,0:T(8,128)S(1)}, f32[56,8,8,128]{3,2,1,0:T(8,128)}, u32[]{:S(2)}) copy-start(f32[56,8,8,128]{3,2,1,0:T(8,128)} %hist_hbm.1) | copy-start | bytes 5505028
  2.1 0.9 %copy-start.1 = (f32[4,8,8,128]{3,2,1,0:T(8,128)S(1)}, f32[4,8,8,128]{3,2,1,0:T(8,128)}, u32[]{:S(2)}) copy-start(f32[4,8,8,128]{3,2,1,0:T(8,128)} %start_hbm.1) | copy-start | bytes 393220
  3.0 0.8 %copy-start.2 = (f32[8,8,128]{2,1,0:T(8,128)S(1)}, f32[8,8,128]{2,1,0:T(8,128)}, u32[]{:S(2)}) copy-start(f32[8,8,128]{2,1,0:T(8,128)} %diag_hbm.1) | copy-start | bytes 98308

commit v2 on v1

v2 whole, which is shorter than its diff:
```python
import functools

import jax
import jax.numpy as jnp
from jax import lax
from jax.experimental import pallas as pl
from jax.experimental.pallas import tpu as pltpu
from jax.sharding import PartitionSpec as P

STEPS = 4
NRHS = 4
HIST = 56
COLS = 20
MESH = pl.DeviceIdType.MESH
F32 = jnp.float32
BF16 = jnp.bfloat16
NT = (((1,), (1,)), ((), ()))
NN = (((1,), (0,)), ((), ()))
HIGH = lax.Precision.HIGHEST
VMEM_BYTES = 66_300_000


def iota(shape, dim):
    return lax.broadcasted_iota(jnp.int32, shape, dim)


def split(value):
    top = value.astype(BF16)
    return top, (value - top.astype(F32)).astype(BF16)


def bdot(left, right, dims):
    return lax.dot_general(left, right, dims, preferred_element_type=F32)


def fdot(left, right, dims):
    return lax.dot_general(left, right, dims, precision=HIGH, preferred_element_type=F32)


def keep_same_row(value):
    same = (iota(value.shape, 0) % 8) == (iota(value.shape, 1) % 8)
    masked = jnp.where(same, value, 0.0)
    return jnp.sum(masked.reshape(value.shape[0] // 8, 8, value.shape[1]), axis=1)


def thirds(value):
    first = value.astype(BF16)
    rest = value - first.astype(F32)
    second = rest.astype(BF16)
    return first, second, (rest - second.astype(F32)).astype(BF16)


class Total:
    def __init__(self, sizes, loc, inp, plane, line, out, send, recv):
        self.nx, self.ny, self.nz = sizes
        self.loc, self.inp, self.plane, self.line, self.out = loc, inp, plane, line, out
        self.send, self.recv = send, recv
        self.ix, self.iy, self.iz = lax.axis_index("gx"), lax.axis_index("gy"), lax.axis_index("gz")
        self.core = lax.rem(self.ix, 2)
        self.iyc = self.ix // 2

    def pair_copy(self, src, dst, number):
        return pltpu.make_async_remote_copy(
            src_ref=src, dst_ref=dst, send_sem=self.send.at[number], recv_sem=self.recv.at[number],
            device_id={"gx": self.ix + 1 - 2 * self.core}, device_id_type=MESH,
        )

    def plane_copies(self):
        nyc, nz = self.nx // 2, self.nz
        for step in range(1, nyc * nz):
            py = lax.rem(self.iyc + step // nz, nyc)
            pz = lax.rem(self.iz + step % nz, nz)
            yield py * nz + pz, self.iyc * nz + self.iz, {"gx": 2 * py + self.core, "gz": pz}, 2 + step

    def line_copies(self):
        for step in range(1, self.ny):
            peer = lax.rem(self.iy + step, self.ny)
            yield peer, self.iy, {"gy": peer}, 2 + (self.nx // 2) * self.nz + step

    def spread(self, copies, buf, base):
        for peer, me, device, number in copies:
            pltpu.make_async_remote_copy(
                src_ref=buf.at[me], dst_ref=buf.at[me], send_sem=self.send.at[number],
                recv_sem=self.recv.at[base + me], device_id=device, device_id_type=MESH,
            ).start()

    def collect(self, copies, buf, base):
        for peer, _, device, number in copies:
            pltpu.make_async_remote_copy(
                src_ref=buf.at[peer], dst_ref=buf.at[peer], send_sem=self.send.at[number],
                recv_sem=self.recv.at[base + peer], device_id=device, device_id_type=MESH,
            ).wait_recv()

    def drain(self, copies, buf, base):
        for peer, me, device, number in copies:
            pltpu.make_async_remote_copy(
                src_ref=buf.at[me], dst_ref=buf.at[me], send_sem=self.send.at[number],
                recv_sem=self.recv.at[base + me], device_id=device, device_id_type=MESH,
            ).wait_send()

    def first(self):
        return self.pair_copy(self.loc.at[1 - self.core], self.inp, 0)

    def last(self):
        return self.pair_copy(self.out.at[self.core], self.out.at[self.core], 1)

    def start_pair(self):
        self.first().start()

    def start_plane(self):
        self.first().wait_recv()
        self.plane[self.iyc * self.nz + self.iz] = self.loc[self.core] + self.inp[...]
        self.spread(self.plane_copies(), self.plane, 2)

    def start_line(self):
        self.collect(self.plane_copies(), self.plane, 2)
        self.line[self.iy] = total_of(self.plane)
        self.spread(self.line_copies(), self.line, 2 + (self.nx // 2) * self.nz)

    def start_share(self):
        self.collect(self.line_copies(), self.line, 2 + (self.nx // 2) * self.nz)
        self.out[self.core] = total_of(self.line)
        self.last().start()

    def result(self):
        other = self.out.at[1 - self.core]
        self.pair_copy(other, other, 1).wait_recv()
        return self.out[0], self.out[1]

    def finish(self):
        self.first().wait_send()
        self.drain(self.plane_copies(), self.plane, 2)
        self.drain(self.line_copies(), self.line, 2 + (self.nx // 2) * self.nz)
        self.last().wait_send()


def total_of(ref):
    parts = [ref[place] for place in range(ref.shape[0])]
    while len(parts) > 1:
        parts = [sum(parts[k:k + 2][1:], parts[k]) for k in range(0, len(parts), 2)]
    return parts[0]


def fold_history(pairs):
    rows = jnp.concatenate(thirds(keep_same_row(pairs)), axis=0)
    pick = ((iota((8 * HIST, 128), 0) // 8) == iota((8 * HIST, 128), 1)).astype(BF16)
    parts = bdot(rows, pick, NN)
    full = parts[0:HIST] + parts[HIST:2 * HIST] + parts[2 * HIST:3 * HIST]
    lane = iota((8, 128), 1)
    tiles = []
    for half in range(2):
        low = 8 * half
        tile = jnp.where(lane < 56, full[low:low + 8], 0.0)
        tile = jnp.where((lane >= 56) & (lane < 96), pltpu.roll(full[16 + low:24 + low], 40, 1), tile)
        tile = jnp.where((lane >= 96) & (lane < 120), pltpu.roll(full[32 + low:40 + low], 64, 1), tile)
        if half == 0:
            tile = jnp.where(lane >= 120, pltpu.roll(full[48:56], 72, 1), tile)
        tiles.append(tile)
    return tiles


def unfold_history(tiles):
    lane = iota((8, 128), 1)
    rows = []
    for first, turn in ((0, 0), (16, 88), (32, 64), (48, 56)):
        for tile in tiles[:1] if first == 48 else tiles:
            turned = tile if turn == 0 else pltpu.roll(tile, turn, 1)
            rows.append(jnp.where((lane >= first) & (lane < HIST), turned, 0.0))
    upper = jnp.concatenate(rows, axis=0)
    right = jnp.where(iota((HIST, 128), 1) >= 16 * (iota((HIST, 128), 0) // 16) + 16, upper, 0.0)
    return upper, right


def fold_basis(pairs):
    rows = keep_same_row(pairs)
    rows = jnp.concatenate([rows, jnp.zeros((128 - HIST - COLS, 8 * COLS), F32)], axis=0)
    rows = jnp.concatenate(thirds(rows), axis=0)
    pick = (iota((24, 8 * COLS), 0) == (iota((24, 8 * COLS), 1) // 8)).astype(BF16)
    parts = bdot(pick, rows, NT)
    full = parts[:, 0:128] + parts[:, 128:256] + parts[:, 256:384]
    lane = iota((8, 128), 1)
    one = jnp.where(lane < HIST, full[0:8], jnp.where(lane >= 64, pltpu.roll(full[8:16], 64, 1), 0.0))
    two = jnp.where(lane < HIST, full[16:24], 0.0)
    for part in range(3):
        first = 64 + 20 * part
        turned = pltpu.roll(full[8 * part:8 * part + 8], first - HIST, 1)
        two = jnp.where((lane >= first) & (lane < first + COLS), turned, two)
    return one, two


def unfold_basis(one, two):
    lane = iota((24, 128), 1)
    coef = jnp.concatenate([one, pltpu.roll(one, 64, 1), two], axis=0)
    own = jnp.concatenate([pltpu.roll(two, 128 - 64 - 20 * part, 1) for part in range(3)], axis=0)
    return jnp.where(lane < HIST, coef, 0.0), jnp.where(lane < COLS, own, 0.0)


def cycle_kernel(
    nx, ny, nz,
    hist_hbm, start_hbm, diag_hbm,
    kept, sums,
    xcat, wbuf, hbuf, ebuf, halo_z, halo_y, halo_x, pack_y, pack_x,
    g_loc, g_inp, g_plane, g_line, g_out,
    c_loc, c_inp, c_plane, c_line, c_out,
    load_sem, hs_sem, hr_sem, g_send, g_recv, c_send, c_recv,
):
    sizes = (nx, ny, nz)
    gsum = Total(sizes, g_loc, g_inp, g_plane, g_line, g_out, g_send, g_recv)
    csum = Total(sizes, c_loc, c_inp, c_plane, c_line, c_out, c_send, c_recv)
    ix, iy, iz = lax.axis_index("gx"), lax.axis_index("gy"), lax.axis_index("gz")
    load_w = pltpu.make_async_copy(start_hbm, wbuf.at[pl.ds(0, NRHS)], load_sem.at[0])
    load_d = pltpu.make_async_copy(diag_hbm, ebuf, load_sem.at[1])
    load_h = pltpu.make_async_copy(hist_hbm, hbuf, load_sem.at[2])
    load_w.start()
    load_d.start()
    load_h.start()

    for which in range(2):
        edge_x = ix == (0 if which == 0 else nx - 1)
        edge_y = iy == (0 if which == 0 else ny - 1)
        edge_z = iz == (0 if which == 0 else nz - 1)

        @pl.when(edge_x)
        def _():
            for level in range(STEPS):
                halo_x[level, which] = jnp.zeros((8, 128), F32)

        @pl.when(edge_y)
        def _():
            for level in range(STEPS):
                halo_y[level, which] = jnp.zeros((32, 128), F32)

        @pl.when(edge_z)
        def _():
            for level in range(STEPS):
                halo_z[level, which] = jnp.zeros((NRHS, 8, 128), F32)

    barrier = pltpu.get_barrier_semaphore()
    greeted = [device for _, _, device, _ in gsum.plane_copies()]
    greeted += [device for _, _, device, _ in gsum.line_copies()]
    greeted += [{"gx": lax.rem(ix + 1, nx)}, {"gx": lax.rem(ix + nx - 1, nx)}]
    for device in greeted:
        pl.semaphore_signal(barrier, inc=1, device_id=device, device_id_type=MESH)

    lane = iota((8, 128), 1)
    row = iota((8, 128), 0)

    def faces(level):
        packed = jnp.zeros((8, 128), F32)
        low_rows, high_rows = [], []
        for f in range(NRHS):
            for z in range(8):
                v = wbuf[NRHS * level + f, z]
                n = 2 * (8 * f + z)
                turned = v if n == 0 else pltpu.roll(v, n, 1)
                packed = jnp.where((lane == n) | (lane == (n + 127) % 128), turned, packed)
                low_rows.append(v[0:1])
                high_rows.append(v[7:8])
        pack_x[level] = packed
        pack_y[level, 0] = jnp.concatenate(low_rows, axis=0)
        pack_y[level, 1] = jnp.concatenate(high_rows, axis=0)

    def halo_copies(level):
        block = pl.ds(NRHS * level, NRHS)
        out = []
        for which, step in ((1, -1), (0, 1)):
            has_x = (ix > 0) if step < 0 else (ix < nx - 1)
            has_y = (iy > 0) if step < 0 else (iy < ny - 1)
            has_z = (iz > 0) if step < 0 else (iz < nz - 1)
            for number, has, axis, me, count, src, dst in (
                (0, has_z, "gz", iz, nz, wbuf.at[block, 0 if step < 0 else 7], halo_z),
                (1, has_y, "gy", iy, ny, pack_y.at[level, 1 - which], halo_y),
                (2, has_x, "gx", ix, nx, pack_x.at[level], halo_x),
            ):
                out.append((
                    has,
                    which,
                    number,
                    pltpu.make_async_remote_copy(
                        src_ref=src,
                        dst_ref=dst.at[level, which],
                        send_sem=hs_sem.at[level, which, number],
                        recv_sem=hr_sem.at[level, which, number],
                        device_id={axis: lax.rem(me + step + count, count)},
                        device_id_type=MESH,
                    ),
                ))
        return out

    def send_halos(level):
        for has, _, _, copy in halo_copies(level):
            @pl.when(has)
            def _():
                copy.start()

    def wait_halos(level):
        for _, which, number, copy in halo_copies(level):
            me, count = ((iz, nz), (iy, ny), (ix, nx))[number]
            has = (me > 0) if which == 0 else (me < count - 1)

            @pl.when(has)
            def _():
                copy.wait_recv()

    def finish_halos(level):
        for has, _, _, copy in halo_copies(level):
            @pl.when(has)
            def _():
                copy.wait_send()

    def keep_split(level):
        for z in range(8):
            block = wbuf[NRHS * level:NRHS * (level + 1), z].reshape(8 * NRHS, 128)
            top, low = split(block)
            rows = pl.ds(8 * (HIST + NRHS * level), 8 * NRHS)
            xcat[rows, 128 * z:128 * (z + 1)] = top
            xcat[rows, 1024 + 128 * z:1024 + 128 * (z + 1)] = low

    def advance(level):
        left, right = halo_x[level, 0], halo_x[level, 1]
        both = jnp.where(lane % 2 == 1, left, right)
        for f in range(NRHS):
            for z in range(8):
                n = 2 * (8 * f + z)
                at = NRHS * level + f
                v = wbuf[at, z]
                turned = both if n == 0 else pltpu.roll(both, 128 - n, 1)
                beside = pltpu.roll(jnp.where(lane == 127, turned, v), 1, 1)
                beside = beside + pltpu.roll(jnp.where(lane == 0, turned, v), 127, 1)
                low = halo_y[level, 0, 8 * f + z:8 * f + z + 1]
                high = halo_y[level, 1, 8 * f + z:8 * f + z + 1]
                beside = beside + jnp.where(row == 0, low, pltpu.roll(v, 1, 0))
                beside = beside + jnp.where(row == 7, high, pltpu.roll(v, 7, 0))
                beside = beside + (halo_z[level, 0, f] if z == 0 else wbuf[at, z - 1])
                beside = beside + (halo_z[level, 1, f] if z == 7 else wbuf[at, z + 1])
                scaled = ebuf[z] * v - beside * (1.0 / 7.0)
                if level > 0:
                    scaled = 2.0 * scaled - wbuf[at - NRHS, z]
                wbuf[at + NRHS, z] = scaled

    load_w.wait()
    faces(0)
    pl.semaphore_wait(barrier, len(greeted))
    send_halos(0)
    load_d.wait()
    ebuf[...] = (ebuf[...] - 1.0) * (1.0 / 7.0)
    load_h.wait()
    for z in range(8):
        top, low = split(hbuf[:, z].reshape(8 * HIST, 128))
        xcat[0:8 * HIST, 128 * z:128 * (z + 1)] = top
        xcat[0:8 * HIST, 1024 + 128 * z:1024 + 128 * (z + 1)] = low

    wait_halos(0)
    advance(0)
    faces(1)
    send_halos(1)
    top, low = xcat[0:8 * HIST, 0:1024], xcat[0:8 * HIST, 1024:2048]
    pairs = bdot(top, top, NT) + bdot(top, low, NT) + bdot(low, top, NT)
    g_loc[0], g_loc[1] = fold_history(pairs)
    gsum.start_pair()

    wait_halos(1)
    advance(1)
    faces(2)
    send_halos(2)
    gsum.start_plane()
    keep_split(0)
    keep_split(1)

    wait_halos(2)
    advance(2)
    faces(3)
    send_halos(3)
    gsum.start_line()
    keep_split(2)
    keep_split(3)

    wait_halos(3)
    advance(3)
    keep_split(4)
    store = pltpu.make_async_copy(xcat, kept, load_sem.at[0])
    store.start()

    wt = xcat[8 * HIST:8 * (HIST + COLS), 0:1024]
    wl = xcat[8 * HIST:8 * (HIST + COLS), 1024:2048]
    xt, xl = xcat[:, 0:1024], xcat[:, 1024:2048]
    pairs = bdot(xt, wt, NT) + bdot(xt, wl, NT) + bdot(xl, wt, NT)
    c_loc[0], c_loc[1] = fold_basis(pairs)
    csum.start_pair()
    csum.start_plane()
    gsum.start_share()
    csum.start_line()
    for level in range(STEPS):
        finish_halos(level)
    sums[2], sums[3] = gsum.result()
    gsum.finish()
    csum.start_share()
    store.wait()
    sums[0], sums[1] = csum.result()
    csum.finish()


def finish_kernel(cells, kept, sums, new_basis, r_factor, xcat, done, load_sem, store_sem):
    load = pltpu.make_async_copy(kept, xcat, load_sem.at[0])
    load.start()
    scale = 1.0 / cells
    one, two, three, four = [sums[k] * scale for k in range(4)]
    gram_h, right_h = unfold_history([three, four])
    lane = iota((24, 128), 1)
    row = iota((24, 128), 0)
    coef, own = unfold_basis(one, two)
    work = fdot(coef[:, 0:HIST], gram_h, NN) + fdot(coef, jnp.concatenate([right_h, jnp.zeros((72, 128), F32)], axis=0), NT)
    wide = jnp.concatenate([coef, jnp.zeros((104, 128), F32)], axis=0)
    gram = fdot(work - 2.0 * coef, wide, NT) + own
    rhs = jnp.where(lane < HIST, -coef, jnp.where(lane - HIST == row, 1.0, 0.0))

    columns = [jnp.broadcast_to(gram[:, k:k + 1], (24, 128)) for k in range(COLS)]
    lower = jnp.zeros((24, 128), F32)
    for j in range(COLS):
        pivot = jnp.broadcast_to(columns[j][j:j + 1], (24, 128))
        inverse = lax.rsqrt(pivot)
        inverse = inverse * (1.5 - 0.5 * pivot * inverse * inverse)
        column = jnp.where(row >= j, columns[j] * inverse, 0.0)
        lower = jnp.where(lane == j, column, lower)
        solved = jnp.broadcast_to(rhs[j:j + 1], (24, 128)) * inverse
        rhs = jnp.where(row == j, solved, rhs - jnp.where(row > j, column * solved, 0.0))
        for k in range(j + 1, COLS):
            columns[k] = columns[k] - column * jnp.broadcast_to(column[k:k + 1], (24, 128))
    square = jnp.concatenate([lower, jnp.zeros((104, 128), F32)], axis=0)
    r_factor[...] = square.T[0:COLS, 0:COLS]

    weights = rhs[0:COLS]
    top, low = split(weights)
    spread = ((iota((128, 8 * (HIST + COLS)), 1) // 8) == iota((128, 8 * (HIST + COLS)), 0)).astype(BF16)
    size = (8 * COLS, 8 * (HIST + COLS))
    same = (iota(size, 0) % 8) == (iota(size, 1) % 8)

    def widen(part):
        wide = bdot(part, spread, NN)
        wide = jnp.broadcast_to(wide[:, None, :], (COLS, 8, size[1])).reshape(size)
        return jnp.where(same, wide, 0.0).astype(BF16)

    top, low = widen(top), widen(low)
    load.wait()
    stores = []
    for part in range(4):
        cols = slice(256 * part, 256 * (part + 1))
        lows = slice(1024 + 256 * part, 1024 + 256 * (part + 1))
        out = bdot(top, xcat[:, cols], NN) + bdot(top, xcat[:, lows], NN) + bdot(low, xcat[:, cols], NN)
        for half in range(2):
            done[:, 2 * part + half] = out[:, 128 * half:128 * (half + 1)].reshape(COLS, 8, 128)
        layers = pl.ds(2 * part, 2)
        stores.append(pltpu.make_async_copy(done.at[:, layers], new_basis.at[:, layers], store_sem.at[part]))
        stores[-1].start()
    for copy in stores:
        copy.wait()


def on_device(nx, ny, nz, history, start, diagonal):
    dma = pltpu.SemaphoreType.DMA
    tiles = lambda *shape: pltpu.VMEM((*shape, 8, 128), F32)
    plane = (nx // 2) * nz
    reduction = [tiles(2), tiles(), tiles(plane), tiles(ny), tiles(2)]
    any_spec = pl.BlockSpec(memory_space=pl.ANY)
    vmem = pl.BlockSpec(memory_space=pltpu.VMEM)
    cells = float(nx * ny * nz * diagonal.size)
    kept, sums = pl.pallas_call(
        functools.partial(cycle_kernel, nx, ny, nz),
        name="cycle",
        out_shape=(
            jax.ShapeDtypeStruct((8 * (HIST + COLS), 2048), BF16),
            jax.ShapeDtypeStruct((4, 8, 128), F32),
        ),
        in_specs=[any_spec] * 3,
        out_specs=(any_spec, vmem),
        scratch_shapes=[
            pltpu.VMEM((8 * (HIST + COLS), 2048), BF16),
            tiles(COLS, 8),
            tiles(HIST, 8),
            tiles(8),
            tiles(STEPS, 2, NRHS),
            pltpu.VMEM((STEPS, 2, 32, 128), F32),
            tiles(STEPS, 2),
            pltpu.VMEM((STEPS, 2, 32, 128), F32),
            tiles(STEPS),
            *reduction,
            *reduction,
            dma((3,)), dma((STEPS, 2, 3)), dma((STEPS, 2, 3)),
            *[dma((2 + plane + ny,))] * 4,
        ],
        compiler_params=pltpu.CompilerParams(
            collective_id=0, has_side_effects=True, vmem_limit_bytes=VMEM_BYTES
        ),
    )(history, start, diagonal)
    return pl.pallas_call(
        functools.partial(finish_kernel, cells),
        name="finish",
        out_shape=(
            jax.ShapeDtypeStruct((COLS, 8, 8, 128), F32),
            jax.ShapeDtypeStruct((COLS, COLS), F32),
        ),
        in_specs=[any_spec, vmem],
        out_specs=(any_spec, vmem),
        scratch_shapes=[pltpu.VMEM((8 * (HIST + COLS), 2048), BF16), tiles(COLS, 8), dma((1,)), dma((4,))],
        compiler_params=pltpu.CompilerParams(vmem_limit_bytes=VMEM_BYTES),
    )(kept, sums)


def solution(mesh):
    return jax.shard_map(
        functools.partial(on_device, mesh.shape["gx"], mesh.shape["gy"], mesh.shape["gz"]),
        mesh=mesh,
        in_specs=(P(None, "gz", "gy", "gx"), P(None, "gz", "gy", "gx"), P("gz", "gy", "gx")),
        out_specs=(P(None, "gz", "gy", "gx"), P()),
        check_vma=False,
    )
```

time: 59.3 us -> 55.5 us (0.936)
  local copies, waits for them, and re-layouts: 3.15 us -> 0 us
    unnamed x6 -> x0, local copies, waits for them, and re-layouts: 3.15 us -> none
    pallas_call x1, Pallas kernels: 52.5 us -> 49.9 us  [on_device(): pl.pallas_call(functools.partial(cycle_kernel, nx, ny, nz), name='cycle',...]
    pallas_call x1, Pallas kernels: 2.74 us -> 4.75 us  [on_device(): pl.pallas_call(functools.partial(finish_kernel, cells), name='finish', ou...]
where the time goes in v2:
time: 55.5 us; the launch traced here: 55.3 us
  Pallas kernels  54.7 us (99%)
  between operations  0.64 us (1%)
    pallas_call x1, Pallas kernels, on_device(): pl.pallas_call(functools.partial(cycle_kernel, nx, ny, nz), name='cycle',...  49.9 us
    pallas_call x1, Pallas kernels, on_device(): pl.pallas_call(functools.partial(finish_kernel, cells), name='finish', ou...  4.75 us

profile of v2, /device:TPU:1, one launch (start us, length us, event | category | flops | bytes accessed | tf_op | source)
XLA Modules:
  0.0 55.3 jit_solution(8591497976148707152)
XLA Ops:
  0.6 49.9 %cycle.1 = (bf16[608,2048]{1,0:T(8,128)(2,1)}, f32[4,8,128]{2,1,0:T(8,128)}) custom-call(f32[56,8,8,128]{3,2,1,0:T(8,128)} %hist_hbm.1, f32[4,8,8,128]{3,2,1,0:T(8,128)} %start_hbm.1, f32[8,8,128]{2,1,0:T(8,128)} %diag_hbm.1), custom_call_target="tpu_custom_call" | custom-call | tf_op jit(solution)/shard_map/cycle/pallas_call | solution.py:467
  50.6 4.7 %finish.1 = (f32[20,8,8,128]{3,2,1,0:T(8,128)}, f32[20,20]{1,0:T(8,128)}) custom-call(bf16[608,2048]{1,0:T(8,128)(2,1)} %get-tuple-element.4.kept, f32[4,8,128]{2,1,0:T(8,128)} %get-tuple-element.5.sums), custom_call_target="tpu_custom_call" | custom-call | tf_op jit(solution)/shard_map/finish/pallas_call | solution.py:495

commit v3 on v2

--- a/solution.py
+++ b/solution.py
@@ -199,7 +199,7 @@
     nx, ny, nz,
     hist_hbm, start_hbm, diag_hbm,
     kept, sums,
-    xcat, wbuf, hbuf, ebuf, halo_z, halo_y, halo_x, pack_y, pack_x,
+    xcat, hbuf, main, side, edge, corner, x_send, x_recv, x_own, e_recv, k_recv, weight_main, weight_side,
     g_loc, g_inp, g_plane, g_line, g_out,
     c_loc, c_inp, c_plane, c_line, c_out,
     load_sem, hs_sem, hr_sem, g_send, g_recv, c_send, c_recv,
@@ -208,176 +208,247 @@
     gsum = Total(sizes, g_loc, g_inp, g_plane, g_line, g_out, g_send, g_recv)
     csum = Total(sizes, c_loc, c_inp, c_plane, c_line, c_out, c_send, c_recv)
     ix, iy, iz = lax.axis_index("gx"), lax.axis_index("gy"), lax.axis_index("gz")
-    load_w = pltpu.make_async_copy(start_hbm, wbuf.at[pl.ds(0, NRHS)], load_sem.at[0])
-    load_d = pltpu.make_async_copy(diag_hbm, ebuf, load_sem.at[1])
+    load_w = pltpu.make_async_copy(start_hbm, main.at[pl.ds(1, NRHS), pl.ds(4, 8)], load_sem.at[0])
+    load_d = pltpu.make_async_copy(diag_hbm, main.at[0, pl.ds(4, 8)], load_sem.at[1])
     load_h = pltpu.make_async_copy(hist_hbm, hbuf, load_sem.at[2])
     load_w.start()
     load_d.start()
     load_h.start()
 
-    for which in range(2):
-        edge_x = ix == (0 if which == 0 else nx - 1)
-        edge_y = iy == (0 if which == 0 else ny - 1)
-        edge_z = iz == (0 if which == 0 else nz - 1)
-
-        @pl.when(edge_x)
-        def _():
-            for level in range(STEPS):
-                halo_x[level, which] = jnp.zeros((8, 128), F32)
-
-        @pl.when(edge_y)
-        def _():
-            for level in range(STEPS):
-                halo_y[level, which] = jnp.zeros((32, 128), F32)
-
-        @pl.when(edge_z)
-        def _():
-            for level in range(STEPS):
-                halo_z[level, which] = jnp.zeros((NRHS, 8, 128), F32)
-
     barrier = pltpu.get_barrier_semaphore()
     greeted = [device for _, _, device, _ in gsum.plane_copies()]
     greeted += [device for _, _, device, _ in gsum.line_copies()]
     greeted += [{"gx": lax.rem(ix + 1, nx)}, {"gx": lax.rem(ix + nx - 1, nx)}]
+    for dy in (1, ny - 1):
+        for dz in (1, nz - 1):
+            greeted.append({"gy": lax.rem(iy + dy, ny), "gz": lax.rem(iz + dz, nz)})
+
+    low_x, high_x = ix == 0, ix == nx - 1
+    low_y, high_y = iy == 0, iy == ny - 1
+    low_z, high_z = iz == 0, iz == nz - 1
+    places = 1 + NRHS
+    zero = jnp.zeros((places, 8, 128), F32)
+    half = jnp.zeros((places, 4, 128), F32)
+    side[0:places, 0] = zero
+    side[0:places, 15] = zero
+    for at, outside in ((0, low_x), (1, high_x)):
+        @pl.when(outside)
+        def _():
+            x_recv[at] = zero
+    for at, outside in ((0, low_y), (1, high_y)):
+        rows = pl.ds(4 - 4 * at, 4)
+
+        @pl.when(outside)
+        def _():
+            for z in range(1, 15):
+                side[0:places, z, rows] = half
+            for third in range(3):
+                k_recv[third, :, rows] = half
+    for at, outside in ((0, low_z), (1, high_z)):
+        @pl.when(outside)
+        def _():
+            e_recv[at] = zero
+            k_recv[1 + at] = zero
+            for z in range(12 * at, 12 * at + 4):
+                main[0:places, z] = zero
+                side[0:places, z] = zero
+
     for device in greeted:
         pl.semaphore_signal(barrier, inc=1, device_id=device, device_id_type=MESH)
 
     lane = iota((8, 128), 1)
     row = iota((8, 128), 0)
 
-    def faces(level):
-        packed = jnp.zeros((8, 128), F32)
-        low_rows, high_rows = [], []
-        for f in range(NRHS):
-            for z in range(8):
-                v = wbuf[NRHS * level + f, z]
-                n = 2 * (8 * f + z)
-                turned = v if n == 0 else pltpu.roll(v, n, 1)
-                packed = jnp.where((lane == n) | (lane == (n + 127) % 128), turned, packed)
-                low_rows.append(v[0:1])
-                high_rows.append(v[7:8])
-        pack_x[level] = packed
-        pack_y[level, 0] = jnp.concatenate(low_rows, axis=0)
-        pack_y[level, 1] = jnp.concatenate(high_rows, axis=0)
-
-    def halo_copies(level):
-        block = pl.ds(NRHS * level, NRHS)
-        out = []
-        for which, step in ((1, -1), (0, 1)):
-            has_x = (ix > 0) if step < 0 else (ix < nx - 1)
-            has_y = (iy > 0) if step < 0 else (iy < ny - 1)
-            has_z = (iz > 0) if step < 0 else (iz < nz - 1)
-            for number, has, axis, me, count, src, dst in (
-                (0, has_z, "gz", iz, nz, wbuf.at[block, 0 if step < 0 else 7], halo_z),
-                (1, has_y, "gy", iy, ny, pack_y.at[level, 1 - which], halo_y),
-                (2, has_x, "gx", ix, nx, pack_x.at[level], halo_x),
-            ):
-                out.append((
-                    has,
-                    which,
-                    number,
-                    pltpu.make_async_remote_copy(
-                        src_ref=src,
-                        dst_ref=dst.at[level, which],
-                        send_sem=hs_sem.at[level, which, number],
-                        recv_sem=hr_sem.at[level, which, number],
-                        device_id={axis: lax.rem(me + step + count, count)},
-                        device_id_type=MESH,
-                    ),
-                ))
+    def there(dx, dy, dz):
+        out = jnp.bool_(True)
+        for step, me, count in ((dx, ix, nx), (dy, iy, ny), (dz, iz, nz)):
+            if step:
+                out = jnp.logical_and(out, me + step >= 0 if step < 0 else me + step < count)
         return out
 
-    def send_halos(level):
-        for has, _, _, copy in halo_copies(level):
-            @pl.when(has)
+    def message(number, dx, dy, dz, src, dst):
+        device = {}
+        for axis, step, me, count in (("gx", dx, ix, nx), ("gy", dy, iy, ny), ("gz", dz, iz, nz)):
+            if step:
+                device[axis] = lax.rem(me + step + count, count)
+        copy = pltpu.make_async_remote_copy(
+            src_ref=src, dst_ref=dst, send_sem=hs_sem.at[number], recv_sem=hr_sem.at[number],
+            device_id=device, device_id_type=MESH,
+        )
+        return there(dx, dy, dz), there(-dx, -dy, -dz), copy
+
+    few = pl.ds(0, places)
+    rows_of = {1: pl.ds(4, 4), -1: pl.ds(0, 4)}
+    first = [message(0, 1, 0, 0, x_send, x_recv.at[0]), message(1, -1, 0, 0, x_send, x_recv.at[1])]
+    first.append(message(2, 0, 0, 1, main.at[few, pl.ds(8, 4)], main.at[few, pl.ds(0, 4)]))
+    first.append(message(3, 0, 0, -1, main.at[few, pl.ds(4, 4)], main.at[few, pl.ds(12, 4)]))
+    second = [message(4, 0, 0, 1, x_own, e_recv.at[0]), message(5, 0, 0, -1, x_own, e_recv.at[1])]
+    for k, dy in enumerate((1, -1)):
+        rows = rows_of[dy]
+        first.append(message(
+            6 + k, 0, dy, 0, main.at[few, pl.ds(4, 8), rows], side.at[few, pl.ds(4, 8), rows]))
+        second.append(message(8 + k, 0, dy, 0, x_own.at[:, rows], k_recv.at[0, :, rows]))
+        for n, dz in enumerate((1, -1)):
+            src = pl.ds(9 if dz > 0 else 4, 3)
+            dst = pl.ds(1 if dz > 0 else 12, 3)
+            first.append(message(
+                10 + 2 * k + n, 0, dy, dz, main.at[few, src, rows], side.at[few, dst, rows]))
+            second.append(message(14 + 2 * k + n, 0, dy, dz, x_own.at[:, rows], k_recv.at[1 + n, :, rows]))
+
+    def send(messages):
+        for sends, _, copy in messages:
+            @pl.when(sends)
             def _():
                 copy.start()
 
-    def wait_halos(level):
-        for _, which, number, copy in halo_copies(level):
-            me, count = ((iz, nz), (iy, ny), (ix, nx))[number]
-            has = (me > 0) if which == 0 else (me < count - 1)
-
-            @pl.when(has)
+    def receive(messages):
+        for _, comes, copy in messages:
+            @pl.when(comes)
             def _():
                 copy.wait_recv()
 
-    def finish_halos(level):
-        for has, _, _, copy in halo_copies(level):
-            @pl.when(has)
+    def leave(messages):
+        for sends, _, copy in messages:
+            @pl.when(sends)
             def _():
                 copy.wait_send()
 
     def keep_split(level):
         for z in range(8):
-            block = wbuf[NRHS * level:NRHS * (level + 1), z].reshape(8 * NRHS, 128)
+            block = main[1 + NRHS * level:1 + NRHS * (level + 1), 4 + z].reshape(8 * NRHS, 128)
             top, low = split(block)
             rows = pl.ds(8 * (HIST + NRHS * level), 8 * NRHS)
             xcat[rows, 128 * z:128 * (z + 1)] = top
             xcat[rows, 1024 + 128 * z:1024 + 128 * (z + 1)] = low
 
+    def turn(value, by, axis):
+        by = by % value.shape[axis]
+        return value if by == 0 else pltpu.roll(value, by, axis)
+
+    inside = lambda outside: jnp.where(outside, 0.0, 1.0).astype(F32)
+    in_z = [inside(low_z) if z < 4 else (inside(high_z) if z > 11 else 1.0) for z in range(16)]
+    in_y = jnp.where(row < 4, inside(high_y), inside(low_y))
+    in_x = jnp.where(lane % 8 < 4, inside(high_x), inside(low_x))
+    in_x = in_x * jnp.where((lane >= 28) & (lane < 92), 1.0, jnp.where((lane >= 92) & (lane < 124), in_z[12], in_z[0]))
+    seventh = 1.0 / 7.0
+
+    def beside_x(value, turned):
+        at = iota(value.shape, 2)
+        left = turn(jnp.where(at == 127, turned, value), 1, 2)
+        return left + turn(jnp.where(at == 0, turned, value), -1, 2)
+
+    def beside_y(inner, outer):
+        at = iota(inner.shape, inner.ndim - 2)
+        inner_low, outer_low = turn(inner, 1, inner.ndim - 2), turn(outer, 1, inner.ndim - 2)
+        inner_high, outer_high = turn(inner, -1, inner.ndim - 2), turn(outer, -1, inner.ndim - 2)
+        return (
+            jnp.where(at == 0, outer_low, inner_low) + jnp.where(at == 7, outer_high, inner_high),
+            jnp.where(at == 0, inner_low, outer_low) + jnp.where(at == 7, inner_high, outer_high),
+        )
+
+    def beside_edge(value, ends):
+        left = jnp.where(lane % 8 == 0, turn(ends, 1, 1), turn(value, 1, 1))
+        right = jnp.where(lane % 8 == 7, turn(ends, -1, 1), turn(value, -1, 1))
+        return left + right + turn(value, 8, 1) + turn(value, -8, 1)
+
+    def spread(value, low, high):
+        return jnp.concatenate([turn(value, -8 * z, 1)[None] for z in range(low, high)], axis=0)
+
+    def ends_of(base, value, low, high):
+        turned = [turn(value[z - low], 8 * z, 1) for z in range(low, high)]
+        for z in range(low, high):
+            base = jnp.where((lane == 8 * z) | (lane == (8 * z + 127) % 128), turned[z - low], base)
+        return base
+
     def advance(level):
-        left, right = halo_x[level, 0], halo_x[level, 1]
-        both = jnp.where(lane % 2 == 1, left, right)
-        for f in range(NRHS):
-            for z in range(8):
-                n = 2 * (8 * f + z)
-                at = NRHS * level + f
-                v = wbuf[at, z]
-                turned = both if n == 0 else pltpu.roll(both, 128 - n, 1)
-                beside = pltpu.roll(jnp.where(lane == 127, turned, v), 1, 1)
-                beside = beside + pltpu.roll(jnp.where(lane == 0, turned, v), 127, 1)
-                low = halo_y[level, 0, 8 * f + z:8 * f + z + 1]
-                high = halo_y[level, 1, 8 * f + z:8 * f + z + 1]
-                beside = beside + jnp.where(row == 0, low, pltpu.roll(v, 1, 0))
-                beside = beside + jnp.where(row == 7, high, pltpu.roll(v, 7, 0))
-                beside = beside + (halo_z[level, 0, f] if z == 0 else wbuf[at, z - 1])
-                beside = beside + (halo_z[level, 1, f] if z == 7 else wbuf[at, z + 1])
-                scaled = ebuf[z] * v - beside * (1.0 / 7.0)
+        more = level < STEPS - 1
+        low, high = level + 1, 15 - level
+
+        def vector(f, carry):
+            at = 1 + NRHS * level + f
+
+            def follow(scaled, ref, *place):
                 if level > 0:
-                    scaled = 2.0 * scaled - wbuf[at - NRHS, z]
-                wbuf[at + NRHS, z] = scaled
+                    scaled = 2.0 * scaled - ref[(at - NRHS, *place)]
+                ref[(at + NRHS, *place)] = scaled
+
+            v, u = main[at, low:high], side[at, low:high]
+            edge_v, corner_v = edge[at], corner[at]
+            turned = spread(edge_v, low, high)
+            if more:
+                turned_u = spread(corner_v, low + 1, high - 1)
+                ends = ends_of(edge_v, v, low, high)
+                side_ends = ends_of(corner_v, u, low, high)
+            across = beside_x(v, turned)
+            if more:
+                across_u = beside_x(u[1:-1], turned_u)
+            near, far = beside_y(v, u)
+            near = near + across + main[at, low - 1:high - 1] + main[at, low + 1:high + 1]
+            follow(main[0, low:high] * v - near * weight_main[low:high], main, slice(low, high))
+            if more:
+                far = far[1:-1] + across_u + side[at, low:high - 2] + side[at, low + 2:high]
+                follow(
+                    side[0, low + 1:high - 1] * u[1:-1] - far * weight_side[low + 1:high - 1],
+                    side, slice(low + 1, high - 1),
+                )
+                near, far = beside_y(edge_v, corner_v)
+                near = near + beside_edge(edge_v, ends)
+                far = far + beside_edge(corner_v, side_ends)
+                follow(edge[0] * edge_v - near * (in_x * seventh), edge)
+                follow(corner[0] * corner_v - far * (in_x * in_y * seventh), corner)
+            return carry
+
+        lax.fori_loop(0, NRHS, vector, 0)
 
     load_w.wait()
-    faces(0)
+    load_d.wait()
+    for place in range(places):
+        packed = jnp.zeros((8, 128), F32)
+        for z in range(4, 12):
+            here = (lane >= 8 * z - 4) & (lane < 8 * z + 4)
+            packed = jnp.where(here, turn(main[place, z], 8 * z, 1), packed)
+        x_send[place] = packed
     pl.semaphore_wait(barrier, len(greeted))
-    send_halos(0)
-    load_d.wait()
-    ebuf[...] = (ebuf[...] - 1.0) * (1.0 / 7.0)
+    send(first)
+
     load_h.wait()
     for z in range(8):
         top, low = split(hbuf[:, z].reshape(8 * HIST, 128))
         xcat[0:8 * HIST, 128 * z:128 * (z + 1)] = top
         xcat[0:8 * HIST, 1024 + 128 * z:1024 + 128 * (z + 1)] = low
-
-    wait_halos(0)
-    advance(0)
-    faces(1)
-    send_halos(1)
+    receive(first[:2])
+    for place in range(places):
+        x_own[place] = jnp.where(lane % 8 >= 4, x_recv[0, place], x_recv[1, place])
+    send(second)
     top, low = xcat[0:8 * HIST, 0:1024], xcat[0:8 * HIST, 1024:2048]
     pairs = bdot(top, top, NT) + bdot(top, low, NT) + bdot(low, top, NT)
     g_loc[0], g_loc[1] = fold_history(pairs)
     gsum.start_pair()
-
-    wait_halos(1)
-    advance(1)
-    faces(2)
-    send_halos(2)
+    keep_split(0)
+
+    receive(first[2:])
+    receive(second)
+    leave(first)
+    own = (lane >= 28) & (lane < 92)
+    for place in range(places):
+        above = turn(jnp.where(lane < 60, e_recv[1, place], e_recv[0, place]), 64, 1)
+        edge[place] = jnp.where(own, x_own[place], above)
+        above = turn(jnp.where(lane < 60, k_recv[2, place], k_recv[1, place]), 64, 1)
+        corner[place] = jnp.where(own, k_recv[0, place], above)
+    for z in range(1, 15):
+        scaled = (main[0, z] - 1.0) * seventh
+        main[0, z] = scaled if 4 <= z < 12 else scaled * in_z[z]
+        scaled = (side[0, z] - 1.0) * (in_y * seventh)
+        side[0, z] = scaled if 4 <= z < 12 else scaled * in_z[z]
+    edge[0] = (edge[0] - 1.0) * (in_x * seventh)
+    corner[0] = (corner[0] - 1.0) * (in_x * in_y * seventh)
+    for z in range(16):
+        weight_main[z] = jnp.full((8, 128), seventh * in_z[z], F32)
+        weight_side[z] = in_y * (seventh * in_z[z])
+    for level in range(STEPS):
+        advance(level)
+        keep_split(level + 1)
     gsum.start_plane()
-    keep_split(0)
-    keep_split(1)
-
-    wait_halos(2)
-    advance(2)
-    faces(3)
-    send_halos(3)
-    gsum.start_line()
-    keep_split(2)
-    keep_split(3)
-
-    wait_halos(3)
-    advance(3)
-    keep_split(4)
     store = pltpu.make_async_copy(xcat, kept, load_sem.at[0])
     store.start()
 
@@ -388,21 +459,24 @@
     c_loc[0], c_loc[1] = fold_basis(pairs)
     csum.start_pair()
     csum.start_plane()
+    gsum.start_line()
+    leave(second)
+    csum.start_line()
     gsum.start_share()
-    csum.start_line()
-    for level in range(STEPS):
-        finish_halos(level)
+    store.wait()
     sums[2], sums[3] = gsum.result()
     gsum.finish()
     csum.start_share()
-    store.wait()
     sums[0], sums[1] = csum.result()
     csum.finish()
 
 
-def finish_kernel(cells, kept, sums, new_basis, r_factor, xcat, done, load_sem, store_sem):
+def finish_kernel(cells, kept, sums_hbm, new_basis, r_out, xcat, sums, done, r_factor, load_sem, store_sem):
+    load_sums = pltpu.make_async_copy(sums_hbm, sums, load_sem.at[1])
+    load_sums.start()
     load = pltpu.make_async_copy(kept, xcat, load_sem.at[0])
     load.start()
+    load_sums.wait()
     scale = 1.0 / cells
     one, two, three, four = [sums[k] * scale for k in range(4)]
     gram_h, right_h = unfold_history([three, four])
@@ -428,6 +502,8 @@
             columns[k] = columns[k] - column * jnp.broadcast_to(column[k:k + 1], (24, 128))
     square = jnp.concatenate([lower, jnp.zeros((104, 128), F32)], axis=0)
     r_factor[...] = square.T[0:COLS, 0:COLS]
+    store_r = pltpu.make_async_copy(r_factor, r_out, store_sem.at[4])
+    store_r.start()
 
     weights = rhs[0:COLS]
     top, low = split(weights)
@@ -454,6 +530,7 @@
         stores[-1].start()
     for copy in stores:
         copy.wait()
+    store_r.wait()
 
 
 def on_device(nx, ny, nz, history, start, diagonal):
@@ -475,17 +552,21 @@
         out_specs=(any_spec, vmem),
         scratch_shapes=[
             pltpu.VMEM((8 * (HIST + COLS), 2048), BF16),
-            tiles(COLS, 8),
             tiles(HIST, 8),
-            tiles(8),
-            tiles(STEPS, 2, NRHS),
-            pltpu.VMEM((STEPS, 2, 32, 128), F32),
-            tiles(STEPS, 2),
-            pltpu.VMEM((STEPS, 2, 32, 128), F32),
-            tiles(STEPS),
+            tiles(1 + COLS, 16),
+            tiles(1 + NRHS * STEPS, 16),
+            tiles(1 + NRHS * STEPS),
+            tiles(1 + NRHS * STEPS),
+            tiles(1 + NRHS),
+            tiles(2, 1 + NRHS),
+            tiles(1 + NRHS),
+            tiles(2, 1 + NRHS),
+            tiles(3, 1 + NRHS),
+            tiles(16),
+            tiles(16),
             *reduction,
             *reduction,
-            dma((3,)), dma((STEPS, 2, 3)), dma((STEPS, 2, 3)),
+            dma((3,)), dma((18,)), dma((18,)),
             *[dma((2 + plane + ny,))] * 4,
         ],
         compiler_params=pltpu.CompilerParams(
@@ -499,9 +580,16 @@
             jax.ShapeDtypeStruct((COLS, 8, 8, 128), F32),
             jax.ShapeDtypeStruct((COLS, COLS), F32),
         ),
-        in_specs=[any_spec, vmem],
-        out_specs=(any_spec, vmem),
-        scratch_shapes=[pltpu.VMEM((8 * (HIST + COLS), 2048), BF16), tiles(COLS, 8), dma((1,)), dma((4,))],
+        in_specs=[any_spec, any_spec],
+        out_specs=(any_spec, any_spec),
+        scratch_shapes=[
+            pltpu.VMEM((8 * (HIST + COLS), 2048), BF16),
+            tiles(4),
+            tiles(COLS, 8),
+            pltpu.VMEM((COLS, COLS), F32),
+            dma((2,)),
+            dma((5,)),
+        ],
         compiler_params=pltpu.CompilerParams(vmem_limit_bytes=VMEM_BYTES),
     )(kept, sums)
 

time: 55.5 us -> 50.4 us (0.908)
  Pallas kernels: 54.7 us -> 49.6 us
    pallas_call x1, Pallas kernels: 49.9 us -> 46 us  [on_device(): pl.pallas_call(functools.partial(cycle_kernel, nx, ny, nz), name='cycle',...]
    pallas_call x1, Pallas kernels: 4.75 us -> 3.55 us  [on_device(): pl.pallas_call(functools.partial(finish_kernel, cells), name='finish', ou...]
where the time goes in v3:
time: 50.4 us; the launch traced here: 50.2 us
  Pallas kernels  49.6 us (98%)
  between operations  0.64 us (1%)
    pallas_call x1, Pallas kernels, on_device(): pl.pallas_call(functools.partial(cycle_kernel, nx, ny, nz), name='cycle',...  46 us
    pallas_call x1, Pallas kernels, on_device(): pl.pallas_call(functools.partial(finish_kernel, cells), name='finish', ou...  3.55 us

profile of v3, /device:TPU:1, one launch (start us, length us, event | category | flops | bytes accessed | tf_op | source)
XLA Modules:
  0.0 50.2 jit_solution(14340708939672062549)
XLA Ops:
  0.6 46.0 %cycle.1 = (bf16[608,2048]{1,0:T(8,128)(2,1)}, f32[4,8,128]{2,1,0:T(8,128)}) custom-call(f32[56,8,8,128]{3,2,1,0:T(8,128)} %hist_hbm.1, f32[4,8,8,128]{3,2,1,0:T(8,128)} %start_hbm.1, f32[8,8,128]{2,1,0:T(8,128)} %diag_hbm.1), custom_call_target="tpu_custom_call" | custom-call | tf_op jit(solution)/shard_map/cycle/pallas_call | solution.py:544
  46.7 3.5 %finish.1 = (f32[20,8,8,128]{3,2,1,0:T(8,128)}, f32[20,20]{1,0:T(8,128)}) custom-call(bf16[608,2048]{1,0:T(8,128)(2,1)} %get-tuple-element.4.kept, f32[4,8,128]{2,1,0:T(8,128)} %get-tuple-element.5.sums_hbm), custom_call_target="tpu_custom_call" | custom-call | tf_op jit(solution)/shard_map/finish/pallas_call | solution.py:576

commit v4 on v3

--- a/solution.py
+++ b/solution.py
@@ -131,7 +131,6 @@
         self.first().wait_send()
         self.drain(self.plane_copies(), self.plane, 2)
         self.drain(self.line_copies(), self.line, 2 + (self.nx // 2) * self.nz)
-        self.last().wait_send()
 
 
 def total_of(ref):
@@ -202,7 +201,7 @@
     xcat, hbuf, main, side, edge, corner, x_send, x_recv, x_own, e_recv, k_recv, weight_main, weight_side,
     g_loc, g_inp, g_plane, g_line, g_out,
     c_loc, c_inp, c_plane, c_line, c_out,
-    load_sem, hs_sem, hr_sem, g_send, g_recv, c_send, c_recv,
+    load_sem, heard, hs_sem, hr_sem, g_send, g_recv, c_send, c_recv,
 ):
     sizes = (nx, ny, nz)
     gsum = Total(sizes, g_loc, g_inp, g_plane, g_line, g_out, g_send, g_recv)
@@ -217,7 +216,9 @@
 
     barrier = pltpu.get_barrier_semaphore()
     greeted = [device for _, _, device, _ in gsum.plane_copies()]
-    greeted += [device for _, _, device, _ in gsum.line_copies()]
+    reach = max(1, ny // 4)
+    for step in range(1, reach + 1):
+        greeted += [{"gy": lax.rem(iy + step, ny)}, {"gy": lax.rem(iy + ny - step, ny)}]
     greeted += [{"gx": lax.rem(ix + 1, nx)}, {"gx": lax.rem(ix + nx - 1, nx)}]
     for dy in (1, ny - 1):
         for dz in (1, nz - 1):
@@ -410,6 +411,10 @@
         x_send[place] = packed
     pl.semaphore_wait(barrier, len(greeted))
     send(first)
+    for side_of, step in ((0, reach), (1, ny - reach)):
+        pl.semaphore_signal(
+            heard.at[side_of], inc=1, device_id={"gy": lax.rem(iy + step, ny)}, device_id_type=MESH
+        )
 
     load_h.wait()
     for z in range(8):
@@ -459,6 +464,8 @@
     c_loc[0], c_loc[1] = fold_basis(pairs)
     csum.start_pair()
     csum.start_plane()
+    for side_of in range(2):
+        pl.semaphore_wait(heard.at[side_of], 1)
     gsum.start_line()
     leave(second)
     csum.start_line()
@@ -466,9 +473,11 @@
     store.wait()
     sums[2], sums[3] = gsum.result()
     gsum.finish()
+    gsum.last().wait_send()
     csum.start_share()
+    csum.finish()
     sums[0], sums[1] = csum.result()
-    csum.finish()
+    csum.last().wait_send()
 
 
 def finish_kernel(cells, kept, sums_hbm, new_basis, r_out, xcat, sums, done, r_factor, load_sem, store_sem):
@@ -566,7 +575,7 @@
             tiles(16),
             *reduction,
             *reduction,
-            dma((3,)), dma((18,)), dma((18,)),
+            dma((3,)), pltpu.SemaphoreType.REGULAR((2,)), dma((18,)), dma((18,)),
             *[dma((2 + plane + ny,))] * 4,
         ],
         compiler_params=pltpu.CompilerParams(

time: 50.4 us -> 48.6 us (0.964)
  Pallas kernels: 49.6 us -> 47.8 us
    pallas_call x1, Pallas kernels: 46 us -> 44.2 us  [on_device(): pl.pallas_call(functools.partial(cycle_kernel, nx, ny, nz), name='cycle',...]
where the time goes in v4:
time: 48.6 us; the launch traced here: 48.4 us
  Pallas kernels  47.8 us (98%)
  between operations  0.64 us (1%)
    pallas_call x1, Pallas kernels, on_device(): pl.pallas_call(functools.partial(cycle_kernel, nx, ny, nz), name='cycle',...  44.2 us
    pallas_call x1, Pallas kernels, on_device(): pl.pallas_call(functools.partial(finish_kernel, cells), name='finish', ou...  3.55 us

profile of v4, /device:TPU:1, one launch (start us, length us, event | category | flops | bytes accessed | tf_op | source)
XLA Modules:
  0.0 48.4 jit_solution(2414562146162547098)
XLA Ops:
  0.6 44.2 %cycle.1 = (bf16[608,2048]{1,0:T(8,128)(2,1)}, f32[4,8,128]{2,1,0:T(8,128)}) custom-call(f32[56,8,8,128]{3,2,1,0:T(8,128)} %hist_hbm.1, f32[4,8,8,128]{3,2,1,0:T(8,128)} %start_hbm.1, f32[8,8,128]{2,1,0:T(8,128)} %diag_hbm.1), custom_call_target="tpu_custom_call" | custom-call | tf_op jit(solution)/shard_map/cycle/pallas_call | solution.py:553
  44.8 3.5 %finish.1 = (f32[20,8,8,128]{3,2,1,0:T(8,128)}, f32[20,20]{1,0:T(8,128)}) custom-call(bf16[608,2048]{1,0:T(8,128)(2,1)} %get-tuple-element.4.kept, f32[4,8,128]{2,1,0:T(8,128)} %get-tuple-element.5.sums_hbm), custom_call_target="tpu_custom_call" | custom-call | tf_op jit(solution)/shard_map/finish/pallas_call | solution.py:585

commit v5 on v4

--- a/solution.py
+++ b/solution.py
@@ -17,7 +17,7 @@
 NT = (((1,), (1,)), ((), ()))
 NN = (((1,), (0,)), ((), ()))
 HIGH = lax.Precision.HIGHEST
-VMEM_BYTES = 66_300_000
+VMEM_BYTES = 56_520_000
 
 
 def iota(shape, dim):
@@ -215,14 +215,36 @@
     load_h.start()
 
     barrier = pltpu.get_barrier_semaphore()
-    greeted = [device for _, _, device, _ in gsum.plane_copies()]
-    reach = max(1, ny // 4)
+    nyc, core = nx // 2, lax.rem(ix, 2)
+    reach = max(1, ny // 8)
+
+    def far_off(dy, dz):
+        return {"gx": 2 * lax.rem(ix // 2 + dy, nyc) + core, "gz": lax.rem(iz + dz, nz)}
+
+    def hops(step, count):
+        return min(step, count - step)
+
+    greeted = [{"gx": lax.rem(ix + 1, nx)}, {"gx": lax.rem(ix + nx - 1, nx)}]
+    for dy in range(nyc):
+        for dz in range(nz):
+            if 1 <= hops(dy, nyc) + hops(dz, nz) <= 2:
+                greeted.append(far_off(dy, dz))
     for step in range(1, reach + 1):
         greeted += [{"gy": lax.rem(iy + step, ny)}, {"gy": lax.rem(iy + ny - step, ny)}]
-    greeted += [{"gx": lax.rem(ix + 1, nx)}, {"gx": lax.rem(ix + nx - 1, nx)}]
     for dy in (1, ny - 1):
         for dz in (1, nz - 1):
             greeted.append({"gy": lax.rem(iy + dy, ny), "gz": lax.rem(iz + dz, nz)})
+
+    def tell(number, device):
+        pl.semaphore_signal(heard.at[number], inc=1, device_id=device, device_id_type=MESH)
+
+    def tell_line(number, step):
+        tell(number, {"gy": lax.rem(iy + step, ny)})
+        tell(number + 1, {"gy": lax.rem(iy + ny - step, ny)})
+
+    def hear(*numbers):
+        for number in numbers:
+            pl.semaphore_wait(heard.at[number], 1)
 
     low_x, high_x = ix == 0, ix == nx - 1
     low_y, high_y = iy == 0, iy == ny - 1
@@ -411,10 +433,11 @@
         x_send[place] = packed
     pl.semaphore_wait(barrier, len(greeted))
     send(first)
-    for side_of, step in ((0, reach), (1, ny - reach)):
-        pl.semaphore_signal(
-            heard.at[side_of], inc=1, device_id={"gy": lax.rem(iy + step, ny)}, device_id_type=MESH
-        )
+    if nyc > 1:
+        tell(0, far_off(nyc // 2, 0))
+    if nz > 1:
+        tell(1, far_off(0, nz // 2))
+    tell_line(2, reach)
 
     load_h.wait()
     for z in range(8):
@@ -425,6 +448,8 @@
     for place in range(places):
         x_own[place] = jnp.where(lane % 8 >= 4, x_recv[0, place], x_recv[1, place])
     send(second)
+    hear(2, 3)
+    tell_line(4, 2 * reach)
     top, low = xcat[0:8 * HIST, 0:1024], xcat[0:8 * HIST, 1024:2048]
     pairs = bdot(top, top, NT) + bdot(top, low, NT) + bdot(low, top, NT)
     g_loc[0], g_loc[1] = fold_history(pairs)
@@ -434,6 +459,8 @@
     receive(first[2:])
     receive(second)
     leave(first)
+    hear(*([0] if nyc > 1 else []), *([1] if nz > 1 else []))
+    gsum.start_plane()
     own = (lane >= 28) & (lane < 92)
     for place in range(places):
         above = turn(jnp.where(lane < 60, e_recv[1, place], e_recv[0, place]), 64, 1)
@@ -453,7 +480,6 @@
     for level in range(STEPS):
         advance(level)
         keep_split(level + 1)
-    gsum.start_plane()
     store = pltpu.make_async_copy(xcat, kept, load_sem.at[0])
     store.start()
 
@@ -463,10 +489,9 @@
     pairs = bdot(xt, wt, NT) + bdot(xt, wl, NT) + bdot(xl, wt, NT)
     c_loc[0], c_loc[1] = fold_basis(pairs)
     csum.start_pair()
+    hear(4, 5)
+    gsum.start_line()
     csum.start_plane()
-    for side_of in range(2):
-        pl.semaphore_wait(heard.at[side_of], 1)
-    gsum.start_line()
     leave(second)
     csum.start_line()
     gsum.start_share()
@@ -480,12 +505,9 @@
     csum.last().wait_send()
 
 
-def finish_kernel(cells, kept, sums_hbm, new_basis, r_out, xcat, sums, done, r_factor, load_sem, store_sem):
-    load_sums = pltpu.make_async_copy(sums_hbm, sums, load_sem.at[1])
-    load_sums.start()
+def finish_kernel(cells, kept, sums, new_basis, r_out, xcat, done, r_factor, load_sem, store_sem):
     load = pltpu.make_async_copy(kept, xcat, load_sem.at[0])
     load.start()
-    load_sums.wait()
     scale = 1.0 / cells
     one, two, three, four = [sums[k] * scale for k in range(4)]
     gram_h, right_h = unfold_history([three, four])
@@ -575,7 +597,7 @@
             tiles(16),
             *reduction,
             *reduction,
-            dma((3,)), pltpu.SemaphoreType.REGULAR((2,)), dma((18,)), dma((18,)),
+            dma((3,)), pltpu.SemaphoreType.REGULAR((6,)), dma((18,)), dma((18,)),
             *[dma((2 + plane + ny,))] * 4,
         ],
         compiler_params=pltpu.CompilerParams(
@@ -589,14 +611,13 @@
             jax.ShapeDtypeStruct((COLS, 8, 8, 128), F32),
             jax.ShapeDtypeStruct((COLS, COLS), F32),
         ),
-        in_specs=[any_spec, any_spec],
+        in_specs=[any_spec, vmem],
         out_specs=(any_spec, any_spec),
         scratch_shapes=[
             pltpu.VMEM((8 * (HIST + COLS), 2048), BF16),
-            tiles(4),
             tiles(COLS, 8),
             pltpu.VMEM((COLS, COLS), F32),
-            dma((2,)),
+            dma((1,)),
             dma((5,)),
         ],
         compiler_params=pltpu.CompilerParams(vmem_limit_bytes=VMEM_BYTES),

time: 48.6 us -> 47.1 us (0.969)
  Pallas kernels: 47.8 us -> 46.3 us
    pallas_call x1, Pallas kernels: 44.2 us -> 42.9 us  [on_device(): pl.pallas_call(functools.partial(cycle_kernel, nx, ny, nz), name='cycle',...]
where the time goes in v5:
time: 47.1 us; the launch traced here: 46.9 us
  Pallas kernels  46.3 us (98%)
  between operations  0.64 us (1%)
    pallas_call x1, Pallas kernels, on_device(): pl.pallas_call(functools.partial(cycle_kernel, nx, ny, nz), name='cycle',...  42.9 us
    pallas_call x1, Pallas kernels, on_device(): pl.pallas_call(functools.partial(finish_kernel, cells), name='finish', ou...  3.44 us

profile of v5, /device:TPU:1, one launch (start us, length us, event | category | flops | bytes accessed | tf_op | source)
XLA Modules:
  0.0 46.9 jit_solution(18318200985836509045)
XLA Ops:
  0.6 42.9 %cycle.1 = (bf16[608,2048]{1,0:T(8,128)(2,1)}, f32[4,8,128]{2,1,0:T(8,128)S(1)}) custom-call(f32[56,8,8,128]{3,2,1,0:T(8,128)} %hist_hbm.1, f32[4,8,8,128]{3,2,1,0:T(8,128)} %start_hbm.1, f32[8,8,128]{2,1,0:T(8,128)} %diag_hbm.1), custom_call_target="tpu_custom_call" | custom-call | tf_op jit(solution)/shard_map/cycle/pallas_call | solution.py:575
  43.5 3.4 %finish.1 = (f32[20,8,8,128]{3,2,1,0:T(8,128)}, f32[20,20]{1,0:T(8,128)}) custom-call(bf16[608,2048]{1,0:T(8,128)(2,1)} %get-tuple-element.4.kept, f32[4,8,128]{2,1,0:T(8,128)S(1)} %get-tuple-element.5.sums), custom_call_target="tpu_custom_call" | custom-call | tf_op jit(solution)/shard_map/finish/pallas_call | solution.py:607

commit v6 on v5

--- a/solution.py
+++ b/solution.py
@@ -421,7 +421,7 @@
                 follow(corner[0] * corner_v - far * (in_x * in_y * seventh), corner)
             return carry
 
-        lax.fori_loop(0, NRHS, vector, 0)
+        lax.fori_loop(0, NRHS, vector, 0, unroll=4)
 
     load_w.wait()
     load_d.wait()
@@ -451,7 +451,7 @@
     hear(2, 3)
     tell_line(4, 2 * reach)
     top, low = xcat[0:8 * HIST, 0:1024], xcat[0:8 * HIST, 1024:2048]
-    pairs = bdot(top, top, NT) + bdot(top, low, NT) + bdot(low, top, NT)
+    pairs = bdot(top, top, NT) + bdot(top, low, NT) + bdot(low, top, NT) + bdot(low, low, NT)
     g_loc[0], g_loc[1] = fold_history(pairs)
     gsum.start_pair()
     keep_split(0)
@@ -486,7 +486,7 @@
     wt = xcat[8 * HIST:8 * (HIST + COLS), 0:1024]
     wl = xcat[8 * HIST:8 * (HIST + COLS), 1024:2048]
     xt, xl = xcat[:, 0:1024], xcat[:, 1024:2048]
-    pairs = bdot(xt, wt, NT) + bdot(xt, wl, NT) + bdot(xl, wt, NT)
+    pairs = bdot(xt, wt, NT) + bdot(xt, wl, NT) + bdot(xl, wt, NT) + bdot(xl, wl, NT)
     c_loc[0], c_loc[1] = fold_basis(pairs)
     csum.start_pair()
     hear(4, 5)

time: 47.1 us -> 45.6 us (0.968)
  Pallas kernels: 46.3 us -> 44.8 us
    pallas_call x1, Pallas kernels: 42.9 us -> 41.3 us  [on_device(): pl.pallas_call(functools.partial(cycle_kernel, nx, ny, nz), name='cycle',...]
where the time goes in v6:
time: 45.6 us; the launch traced here: 45.4 us
  Pallas kernels  44.8 us (98%)
  between operations  0.64 us (1%)
    pallas_call x1, Pallas kernels, on_device(): pl.pallas_call(functools.partial(cycle_kernel, nx, ny, nz), name='cycle',...  41.3 us
    pallas_call x1, Pallas kernels, on_device(): pl.pallas_call(functools.partial(finish_kernel, cells), name='finish', ou...  3.44 us

profile of v6, /device:TPU:1, one launch (start us, length us, event | category | flops | bytes accessed | tf_op | source)
XLA Modules:
  0.0 45.4 jit_solution(11998664386123352253)
XLA Ops:
  0.6 41.3 %cycle.1 = (bf16[608,2048]{1,0:T(8,128)(2,1)}, f32[4,8,128]{2,1,0:T(8,128)S(1)}) custom-call(f32[56,8,8,128]{3,2,1,0:T(8,128)} %hist_hbm.1, f32[4,8,8,128]{3,2,1,0:T(8,128)} %start_hbm.1, f32[8,8,128]{2,1,0:T(8,128)} %diag_hbm.1), custom_call_target="tpu_custom_call" | custom-call | tf_op jit(solution)/shard_map/cycle/pallas_call | solution.py:575
  42.0 3.4 %finish.1 = (f32[20,8,8,128]{3,2,1,0:T(8,128)}, f32[20,20]{1,0:T(8,128)}) custom-call(bf16[608,2048]{1,0:T(8,128)(2,1)} %get-tuple-element.4.kept, f32[4,8,128]{2,1,0:T(8,128)S(1)} %get-tuple-element.5.sums), custom_call_target="tpu_custom_call" | custom-call | tf_op jit(solution)/shard_map/finish/pallas_call | solution.py:607

commit v7 on v6

--- a/solution.py
+++ b/solution.py
@@ -35,6 +35,11 @@
 
 def fdot(left, right, dims):
     return lax.dot_general(left, right, dims, precision=HIGH, preferred_element_type=F32)
+
+
+def both_products(left, right):
+    swapped = jnp.concatenate([right[:, 1024:2048], right[:, 0:1024]], axis=1)
+    return bdot(left, right, NT) + bdot(left, swapped, NT)
 
 
 def keep_same_row(value):
@@ -450,8 +455,7 @@
     send(second)
     hear(2, 3)
     tell_line(4, 2 * reach)
-    top, low = xcat[0:8 * HIST, 0:1024], xcat[0:8 * HIST, 1024:2048]
-    pairs = bdot(top, top, NT) + bdot(top, low, NT) + bdot(low, top, NT) + bdot(low, low, NT)
+    pairs = both_products(xcat[0:8 * HIST], xcat[0:8 * HIST])
     g_loc[0], g_loc[1] = fold_history(pairs)
     gsum.start_pair()
     keep_split(0)
@@ -483,10 +487,7 @@
     store = pltpu.make_async_copy(xcat, kept, load_sem.at[0])
     store.start()
 
-    wt = xcat[8 * HIST:8 * (HIST + COLS), 0:1024]
-    wl = xcat[8 * HIST:8 * (HIST + COLS), 1024:2048]
-    xt, xl = xcat[:, 0:1024], xcat[:, 1024:2048]
-    pairs = bdot(xt, wt, NT) + bdot(xt, wl, NT) + bdot(xl, wt, NT) + bdot(xl, wl, NT)
+    pairs = both_products(xcat[...], xcat[8 * HIST:8 * (HIST + COLS)])
     c_loc[0], c_loc[1] = fold_basis(pairs)
     csum.start_pair()
     hear(4, 5)

time: 45.6 us -> 45.6 us (level)
  no operation moved by 1% of the time
where the time goes in v7:
time: 45.6 us; the launch traced here: 45.4 us
  Pallas kernels  44.8 us (98%)
  between operations  0.64 us (1%)
    pallas_call x1, Pallas kernels, on_device(): pl.pallas_call(functools.partial(cycle_kernel, nx, ny, nz), name='cycle',...  41.3 us
    pallas_call x1, Pallas kernels, on_device(): pl.pallas_call(functools.partial(finish_kernel, cells), name='finish', ou...  3.44 us

profile of v7, /device:TPU:1, one launch (start us, length us, event | category | flops | bytes accessed | tf_op | source)
XLA Modules:
  0.0 45.4 jit_solution(13560471945294681005)
XLA Ops:
  0.6 41.3 %cycle.1 = (bf16[608,2048]{1,0:T(8,128)(2,1)}, f32[4,8,128]{2,1,0:T(8,128)S(1)}) custom-call(f32[56,8,8,128]{3,2,1,0:T(8,128)} %hist_hbm.1, f32[4,8,8,128]{3,2,1,0:T(8,128)} %start_hbm.1, f32[8,8,128]{2,1,0:T(8,128)} %diag_hbm.1), custom_call_target="tpu_custom_call" | custom-call | tf_op jit(solution)/shard_map/cycle/pallas_call | solution.py:576
  42.0 3.4 %finish.1 = (f32[20,8,8,128]{3,2,1,0:T(8,128)}, f32[20,20]{1,0:T(8,128)}) custom-call(bf16[608,2048]{1,0:T(8,128)(2,1)} %get-tuple-element.4.kept, f32[4,8,128]{2,1,0:T(8,128)S(1)} %get-tuple-element.5.sums), custom_call_target="tpu_custom_call" | custom-call | tf_op jit(solution)/shard_map/finish/pallas_call | solution.py:608
